TPU v7x, 512 devices: a whole 4x4x16 slice. The times are simulated.
512 devices in a mesh: section: 16 (over z), req: 4 (over y), tp: 8 (over x, core).
Axes of the slice: x: 4, y: 4, z: 16, core: 2. Of those that a mesh axis runs over, the one named last changes fastest.
Arguments:
- hidden: bfloat16 [4, 16, 64, 8192], P(None, 'section', 'req', 'tp'), may hold values from -6 to 6
- norm_gain: bfloat16 [16, 8192], P('section', 'tp'), may hold values from 0.099609375 to 1.8984375
- w_kv: bfloat16 [16, 8192, 2, 1024], P('section', None, None, 'tp'), may hold values from -0.0625 to 0.0625
- queries: bfloat16 [4, 16, 64, 8192], P(None, 'section', 'req', 'tp'), may hold values from -120 to 120
- cache_kv: bfloat16 [16, 64, 2, 128, 1024], P('section', 'req', None, None, 'tp'), may hold values from -4 to 4
- exits: int32 [4, 64], P(None, 'req'), may hold values from 0 to 16, as said below
- lengths: int32 [64], P('req'), may hold values from 2 to 124, as said below
Outputs:
- attn_out: bfloat16 [4, 16, 64, 8192], P(None, 'section', 'req', 'tp')
- new_kv: bfloat16 [4, 16, 64, 2, 1024], P(None, 'section', 'req', None, 'tp')
Inputs may be any that keep to these rules, and one draw needn't show every extreme that they name: `exits`: in each step, among the 16 requests of each aligned block, no layer below 16 is named by more than 2 requests, some layer below 16 is named by exactly 2, and some request names 16. `lengths`: every aligned block of 16 requests holds a request of length 124.
All inputs are finite; a program needn't handle non-finite values.
Results may differ from a plain program's by a relative error of at most 0.0056.
Values may be sent and summed in bfloat16 or wider, within the bound.
No kernel may reach another device: no remote copies, remote signals or barrier semaphores. Data moves between devices by JAX's collectives and lax.ppermute only.
A program may use at most 64 MiB of HBM per device.

v0:
```python
import jax
import jax.numpy as jnp
from jax import lax
from jax.sharding import PartitionSpec as P

D = 8192
HEAD = 128


EPSILON = 1e-05
ROPE_BASE = 500000.0


def carried_in(x, axis, combine, identity):
    count, place = (lax.axis_size(axis), lax.axis_index(axis))
    everything = lax.all_gather(x, axis)
    start = jnp.broadcast_to(jnp.asarray(identity, x.dtype), x.shape)

    def lap(k, before):
        reached = k < place
        new = combine(before, everything[k])
        return jnp.where(reached, new, before)

    return lax.fori_loop(0, count, lap, start)


def apply_rotary(key_heads, positions):
    half_width = key_heads.shape[-1] // 2
    exponent = jnp.arange(half_width, dtype=jnp.float32) * (2.0 / key_heads.shape[-1])
    frequency = ROPE_BASE ** (-exponent)
    angles = positions.astype(jnp.float32)[..., None, None] * frequency
    cosine = jnp.cos(angles)
    sine_part = jnp.sin(angles)
    lower = key_heads[..., :half_width]
    upper = key_heads[..., half_width:]
    return jnp.concatenate(
        [lower * cosine - upper * sine_part, upper * cosine + lower * sine_part], axis=-1
    )


def add_sources(earlier_part, later_part):
    return earlier_part + later_part


def local(hidden, norm_gain, w_kv, queries, cache_kv, exits, lengths):
    num_steps = hidden.shape[0]
    local_reqs = hidden.shape[2]
    section_index = lax.axis_index("section")
    own_rows = hidden[:, 0]
    leaving = exits == section_index
    outgoing = jnp.where(leaving[..., None], own_rows, jnp.zeros_like(own_rows))
    arrived = carried_in(outgoing, "section", add_sources, jnp.zeros_like(outgoing))
    source_rows = jnp.where((exits < section_index)[..., None], arrived, own_rows).astype(
        jnp.bfloat16
    )
    flat_count = num_steps * local_reqs
    rows_float = source_rows.astype(jnp.float32)
    squares = lax.psum(jnp.sum(rows_float * rows_float, axis=-1), "tp")
    inverse = lax.rsqrt(squares / D + EPSILON)
    normed_part = (rows_float * inverse[..., None] * norm_gain[0].astype(jnp.float32)).astype(
        jnp.bfloat16
    )
    normed_part = normed_part.reshape(flat_count, normed_part.shape[-1])
    normed = lax.all_gather(normed_part, "tp", axis=1, tiled=True)
    kv_local = w_kv.shape[-1]
    flat_weight = w_kv[0].reshape(w_kv.shape[1], 2 * kv_local)
    kv_pairs = jnp.dot(normed, flat_weight, preferred_element_type=jnp.float32)
    local_heads = kv_local // HEAD
    kv_pairs = kv_pairs.reshape(num_steps, local_reqs, 2, local_heads, HEAD)
    positions = lengths[None, :] + jnp.arange(num_steps, dtype=jnp.int32)[:, None]
    new_keys = apply_rotary(kv_pairs[:, :, 0], positions).astype(jnp.bfloat16)
    new_values = kv_pairs[:, :, 1].astype(jnp.bfloat16)
    fresh_kv = jnp.stack([new_keys, new_values], axis=2).reshape(num_steps, local_reqs, 2, kv_local)
    kv_cache = cache_kv[0]
    cache_len = kv_cache.shape[2]
    slot_ids = jnp.arange(cache_len, dtype=jnp.int32)
    for step_index in range(num_steps):
        written = slot_ids[None, :] == positions[step_index][:, None]
        kv_cache = jnp.where(
            written[:, None, :, None], fresh_kv[step_index][:, :, None, :], kv_cache
        )
    all_keys = kv_cache[:, 0].reshape(local_reqs, cache_len, local_heads, HEAD)
    all_values = kv_cache[:, 1].reshape(local_reqs, cache_len, local_heads, HEAD)
    groups = queries.shape[-1] // kv_local
    query_heads = queries[:, 0].reshape(num_steps, local_reqs, local_heads, groups, HEAD)
    scores = jnp.einsum(
        "trkgd,rckd->trkgc", query_heads, all_keys, preferred_element_type=jnp.float32
    ) * HEAD ** (-0.5)
    visible = slot_ids[None, None, :] <= positions[:, :, None]
    scores = jnp.where(visible[:, :, None, None, :], scores, -1e30)
    top_score = jnp.max(scores, axis=-1, keepdims=True)
    weights = jnp.exp(scores - top_score)
    weights = (weights / jnp.sum(weights, axis=-1, keepdims=True)).astype(jnp.bfloat16)
    attended = jnp.einsum(
        "trkgc,rckd->trkgd", weights, all_values, preferred_element_type=jnp.float32
    )
    live_mask = (section_index < exits).astype(jnp.float32)
    attended = attended * live_mask[:, :, None, None, None]
    attended = attended.reshape(num_steps, 1, local_reqs, queries.shape[-1]).astype(jnp.bfloat16)
    return (attended, fresh_kv[:, None])


def solution(mesh):
    placed = (
        P(None, "section", "req", "tp"),
        P("section", "tp"),
        P("section", None, None, "tp"),
        P(None, "section", "req", "tp"),
        P("section", "req", None, None, "tp"),
        P(None, "req"),
        P("req"),
    )
    return jax.shard_map(
        local,
        mesh=mesh,
        in_specs=placed,
        out_specs=(P(None, "section", "req", "tp"), P(None, "section", "req", None, "tp")),
        check_vma=False,
    )
```

profile of v0, /device:TPU:1, one launch (start us, length us, event | category | flops | bytes accessed | tf_op | source)
XLA Modules:
  0.0 160.9 jit_solution(7580655298327867797)
XLA Ops:
  7.9 1.6 %bitcast_select_fusion.2 = bf16[1,4,16,1024]{3,2,1,0:T(8,128)(2,1)} fusion(bf16[4,1,16,1024]{3,2,1,0:T(8,128)(2,1)} %param.9, pred[4,16]{1,0:T(4,128)(4,1)S(1)} %get-tuple-element.117), kind=kLoop, calls=%fused_computation.25 | loop fusion | flops 65536 | bytes 262208 | tf_op jit(solution)/shard_map/jit(_where)/select_n | solution.py:51
  10.3 69.1 %all-gather.3.cloned.1.call-done = bf16[16,4,16,1024]{3,2,1,0:T(8,128)(2,1)} async-done(((bf16[1,4,16,1024]{3,2,1,0:T(8,128)(2,1)}), bf16[16,4,16,1024]{3,2,1,0:T(8,128)(2,1)}) %all-gather.3.cloned.1.call-update) | async-done | bytes 2097168 | tf_op jit(solution)/shard_map/all_gather | solution.py:16
  79.4 15.6 %while.14 = (s32[]{:T(128)}, bf16[4,16,1024]{2,1,0:T(8,128)(2,1)S(1)}, s32[]{:T(128)}, bf16[16,4,16,1024]{3,2,1,0:T(8,128)(2,1)}, s32[]{:T(128)}, /*index=5*/s32[]{:T(128)}) while((s32[]{:T(128)}, bf16[4,16,1024]{2,1,0:T(8,128)(2,1)S(1)}, s32[]{:T(128)}, bf16[16,4,16,1024]{3,2,1,0:T(8,128)(2,1)}, s32[]{:T(128)}, ...), condition=%wide.region_1.2_spmd.clone, body=%wide.region_0.1_spmd.clone.sunk | while | flops 196612 | bytes 393309 | solution.py:24
  80.3 1.0 add_select_fusion.2
  81.3 1.0 add_select_fusion.2
  82.3 1.0 add_select_fusion.2
  83.3 1.0 add_select_fusion.2
  84.2 1.0 add_select_fusion.2
  85.2 1.0 add_select_fusion.2
  87.2 1.0 add_select_fusion.2
  88.1 1.0 add_select_fusion.2
  89.1 1.0 add_select_fusion.2
  90.1 1.0 add_select_fusion.2
  91.1 1.0 add_select_fusion.2
  92.0 1.0 add_select_fusion.2
  93.0 1.0 add_select_fusion.2
  94.9 1.1 fusion.7
  96.0 21.6 %psum.7 = f32[4,16]{1,0:T(4,128)S(1)} all-reduce(f32[4,16]{1,0:T(4,128)S(1)} %fusion.7), channel_id=1, replica_groups=mesh['section'=16,'req'=4,'tp'=8] {'tp'}, use_global_device_ids=true, to_apply=%region_3.4 | all-reduce | flops 64 | bytes 512 | tf_op jit(solution)/shard_map/psum | solution.py:58
  117.7 1.7 %fusion.9 = bf16[4,16,1024]{2,1,0:T(8,128)(2,1)} fusion(f32[1024]{0:T(1024)S(1)} %bitcast.122, f32[4,16]{1,0:T(4,128)S(1)} %add_rsqrt_fusion, bf16[4,16,1024]{2,1,0:T(8,128)(2,1)S(1)} %get-tuple-element.81, bf16[4,1,16,1024]{3,2,1,0:T(8,128)(2,1)} %param.9, pred[4,16]{1,0:T(4,128)(4,1)S(1)} %get-tuple-element.116), kind=kLoop, calls=%fused_computation.19 | loop fusion | flops 327680 | bytes 397632 | tf_op jit(solution)/shard_map/convert_element_type | solution.py:60
  119.4 4.7 %copy.39 = bf16[1024,8,2,128]{3,1,2,0:T(8,128)(2,1)} copy(bf16[1024,8,2,128]{3,2,1,0:T(2,128)(2,1)} %bitcast.117) | data formatting | bytes 8388608
  124.1 6.5 %copy.18 = bf16[256,8192]{1,0:T(8,128)(2,1)} copy(bf16[256,8192]{0,1:T(8,128)(2,1)} %bitcast.116) | data formatting | bytes 8388608 | tf_op jit(solution)/shard_map/dot_general | solution.py:67
  131.1 14.7 %all-gather.5.cloned.1.call-done = bf16[64,8192]{1,0:T(8,128)(2,1)} async-done(((bf16[64,1024]{1,0:T(8,128)(2,1)}), bf16[64,8192]{1,0:T(8,128)(2,1)}) %all-gather.5.cloned.1.call-update) | async-done | bytes 1048592 | tf_op jit(solution)/shard_map/all_gather | solution.py:64
  145.7 4.0 %convolution_bitcast_fusion.1 = f32[4,16,2,1,128]{4,1,2,0,3:T(8,128)S(1)} fusion(bf16[4,16,8192,1]{2,1,3,0:T(8,128)(2,1)} %bitcast.123, bf16[2,128,8192,1]{2,1,0,3:T(8,128)(2,1)} %bitcast.118), kind=kOutput, calls=%fused_computation.8 | convolution fusion | flops 268435456 | bytes 5308416 | tf_op jit(solution)/shard_map/dot_general | solution.py:67
  150.1 1.4 fusion.6
  (38 shorter events, 7.7 us)
Async XLA Ops:
  7.2 72.2 %all-gather.3.cloned.1.call-start = ((), (), s32[]{:S(2)}) async-start(), calls=%async_computation | async-start | bytes 2228224 | tf_op jit(solution)/shard_map/all_gather | solution.py:16
  9.6 136.2 %all-gather.5.cloned.1.call-start = ((), (), s32[]{:S(2)}) async-start(), calls=%async_computation.1 | async-start | bytes 1179648 | tf_op jit(solution)/shard_map/all_gather | solution.py:64
  124.1 6.5 %copy-start.2 = (s32[16]{0:T(128)S(1)}, s32[16]{0:T(128)}, u32[]{:S(2)}) copy-start(s32[16]{0:T(128)} %param.15) | copy-start | bytes 196
  124.1 6.6 %copy-start.1 = (bf16[4,1,16,1024]{3,2,1,0:T(8,128)(2,1)S(1)}, bf16[4,1,16,1024]{3,2,1,0:T(8,128)(2,1)}, u32[]{:S(2)}) copy-start(bf16[4,1,16,1024]{3,2,1,0:T(8,128)(2,1)} %param.12) | copy-start | bytes 393220
  145.7 4.4 %copy-start = (bf16[1,16,2,128,128]{4,3,2,1,0:T(8,128)(2,1)S(1)}, bf16[1,16,2,128,128]{4,3,2,1,0:T(8,128)(2,1)}, u32[]{:S(2)}) copy-start(bf16[1,16,2,128,128]{4,3,2,1,0:T(8,128)(2,1)} %param.13) | copy-start | bytes 3145732
Sparse Core Ops, SparseCore 0:
  10.6 68.7 all-gather.2
  119.5 26.1 all-gather.4
where the time goes:
time: 162 us; the launch traced here: 161 us
  waiting for transfers between devices  83.8 us (52%)
  other arithmetic  23.4 us (14%)
  blocking collectives  21.6 us (13%)
  between operations  14.1 us (9%)
  local copies, waits for them, and re-layouts  12.8 us (8%)
  matrix products  4.78 us (3%)
    all_gather x1, waiting for transfers between devices, carried_in(): everything = lax.all_gather(x, axis)  69.1 us
    psum x1, blocking collectives, local(): squares = lax.psum(jnp.sum(rows_float * rows_float, axis=-1), 'tp')  21.6 us
    select_n x16, other arithmetic, lap(): return jnp.where(reached, new, before)  15.2 us
    all_gather x1, waiting for transfers between devices, local(): normed = lax.all_gather(normed_part, 'tp', axis=1, tiled=True)  14.7 us
    dot_general x1, local copies, waits for them, and re-layouts, local(): kv_pairs = jnp.dot(normed, flat_weight, preferred_element_type=jnp.float32)  6.46 us
    unnamed x10, local copies, waits for them, and re-layouts  6.07 us
    dot_general x1, matrix products, local(): kv_pairs = jnp.dot(normed, flat_weight, preferred_element_type=jnp.float32)  3.98 us
  transfers between devices with their start and end apart: 2, of which 2 were waited for; matrix products, arithmetic and copies ran while one was open for 8% of the time, Pallas kernels for 0%

commit v1 on v0

--- a/solution.py
+++ b/solution.py
@@ -5,23 +5,11 @@
 
 D = 8192
 HEAD = 128
+EXIT_CAP = 2
 
 
 EPSILON = 1e-05
 ROPE_BASE = 500000.0
-
-
-def carried_in(x, axis, combine, identity):
-    count, place = (lax.axis_size(axis), lax.axis_index(axis))
-    everything = lax.all_gather(x, axis)
-    start = jnp.broadcast_to(jnp.asarray(identity, x.dtype), x.shape)
-
-    def lap(k, before):
-        reached = k < place
-        new = combine(before, everything[k])
-        return jnp.where(reached, new, before)
-
-    return lax.fori_loop(0, count, lap, start)
 
 
 def apply_rotary(key_heads, positions):
@@ -38,33 +26,63 @@
     )
 
 
-def add_sources(earlier_part, later_part):
-    return earlier_part + later_part
+def spread(x, axis, count, groups=None):
+    return lax.all_to_all(
+        jnp.broadcast_to(x[None], (count,) + x.shape), axis, 0, 0, axis_index_groups=groups
+    )
+
+
+def source_rows(own_rows, exits, section_index, sections):
+    steps, reqs, width = own_rows.shape
+    rows = steps * reqs
+    same = exits[:, :, None] == exits[:, None, :]
+    earlier = jnp.arange(reqs)[None, None, :] < jnp.arange(reqs)[None, :, None]
+    rank = jnp.sum((same & earlier).astype(jnp.int32), axis=-1)
+    step_of = jnp.arange(steps, dtype=jnp.int32)[:, None]
+    place = (step_of * EXIT_CAP + rank).reshape(rows)
+    flat_exits = exits.reshape(rows)
+    slots = steps * EXIT_CAP
+    own_flat = own_rows.reshape(rows, width)
+    slot_ids = jnp.arange(slots, dtype=jnp.int32)
+    pick = (slot_ids[:, None] == place[None, :]) & (flat_exits == section_index)[None, :]
+    outgoing = jnp.dot(
+        pick.astype(jnp.bfloat16), own_flat, preferred_element_type=jnp.float32
+    ).astype(jnp.bfloat16)
+    arrived = spread(outgoing, "section", sections).reshape(sections * slots, width)
+    gone = flat_exits < section_index
+    all_ids = jnp.arange(sections * slots, dtype=jnp.int32)
+    take = (all_ids[None, :] == (flat_exits * slots + place)[:, None]) & gone[:, None]
+    taken = jnp.dot(
+        take.astype(jnp.bfloat16), arrived, preferred_element_type=jnp.float32
+    ).astype(jnp.bfloat16)
+    return jnp.where(gone[:, None], taken, own_flat)
 
 
 def local(hidden, norm_gain, w_kv, queries, cache_kv, exits, lengths):
     num_steps = hidden.shape[0]
     local_reqs = hidden.shape[2]
+    rows = num_steps * local_reqs
+    sections = lax.axis_size("section")
     section_index = lax.axis_index("section")
-    own_rows = hidden[:, 0]
-    leaving = exits == section_index
-    outgoing = jnp.where(leaving[..., None], own_rows, jnp.zeros_like(own_rows))
-    arrived = carried_in(outgoing, "section", add_sources, jnp.zeros_like(outgoing))
-    source_rows = jnp.where((exits < section_index)[..., None], arrived, own_rows).astype(
-        jnp.bfloat16
-    )
-    flat_count = num_steps * local_reqs
-    rows_float = source_rows.astype(jnp.float32)
-    squares = lax.psum(jnp.sum(rows_float * rows_float, axis=-1), "tp")
+    parts = lax.axis_size("tp")
+    chips = parts // 2
+    core = lax.axis_index("tp") % 2
+    source = source_rows(hidden[:, 0], exits, section_index, sections)
+    sent = jnp.concatenate([source, jnp.broadcast_to(norm_gain, (8, norm_gain.shape[1]))], axis=0)
+    same_core = [[2 * x + c for x in range(chips)] for c in range(2)]
+    mine = spread(sent, "tp", chips, same_core)
+    other = lax.ppermute(mine, "tp", [(i, i ^ 1) for i in range(parts)])
+    even = jnp.where(core == 0, mine, other)
+    odd = jnp.where(core == 0, other, mine)
+    both = jnp.stack([even, odd], axis=1).reshape(parts, rows + 8, D // parts)
+    raw = both[:, :rows].astype(jnp.float32)
+    gain = both[:, rows].astype(jnp.float32)
+    squares = jnp.sum(raw * raw, axis=(0, 2))
     inverse = lax.rsqrt(squares / D + EPSILON)
-    normed_part = (rows_float * inverse[..., None] * norm_gain[0].astype(jnp.float32)).astype(
-        jnp.bfloat16
-    )
-    normed_part = normed_part.reshape(flat_count, normed_part.shape[-1])
-    normed = lax.all_gather(normed_part, "tp", axis=1, tiled=True)
+    normed = (raw * inverse[None, :, None] * gain[:, None, :]).astype(jnp.bfloat16)
     kv_local = w_kv.shape[-1]
-    flat_weight = w_kv[0].reshape(w_kv.shape[1], 2 * kv_local)
-    kv_pairs = jnp.dot(normed, flat_weight, preferred_element_type=jnp.float32)
+    weight = w_kv[0].reshape(parts, D // parts, 2 * kv_local)
+    kv_pairs = jnp.einsum("prd,pdk->rk", normed, weight, preferred_element_type=jnp.float32)
     local_heads = kv_local // HEAD
     kv_pairs = kv_pairs.reshape(num_steps, local_reqs, 2, local_heads, HEAD)
     positions = lengths[None, :] + jnp.arange(num_steps, dtype=jnp.int32)[:, None]

time: 162 us -> 82.9 us (0.51)
  waiting for transfers between devices: 83.8 us -> 19.5 us
  starting transfers between devices: 0.08 us -> 28.6 us
  blocking collectives: 21.6 us -> 0 us
  other arithmetic: 23.4 us -> 6.36 us
  between operations: 14.1 us -> 0.85 us
  local copies, waits for them, and re-layouts: 12.8 us -> 19.4 us
  matrix products: 4.78 us -> 7.54 us
    all_gather x2 -> x0, waiting for transfers between devices: 83.7 us -> none  [the longest x1 69.1 us: carried_in(): everything = lax.all_gather(x, axis)]
    psum x1 -> x0, blocking collectives: 21.6 us -> none  [local(): squares = lax.psum(jnp.sum(rows_float * rows_float, axis=-1), 'tp')]
    all_to_all x0 -> x2, starting transfers between devices: none -> 19.7 us  [spread(): lax.all_to_all(jnp.broadcast_to(x[None], (count,) + x.shape), axis, 0, 0,...]
    all_to_all x0 -> x2, waiting for transfers between devices: none -> 19.5 us  [spread(): lax.all_to_all(jnp.broadcast_to(x[None], (count,) + x.shape), axis, 0, 0,...]
    select_n x17 -> x0, other arithmetic: 16.9 us -> none  [the longest x16 15.2 us: lap(): return jnp.where(reached, new, before)]
    another operation x0 -> x2, local copies, waits for them, and re-layouts: none -> 14.4 us  [local(): weight = w_kv[0].reshape(parts, D // parts, 2 * kv_local)]
    ppermute x0 -> x1, starting transfers between devices: none -> 8.89 us  [local(): other = lax.ppermute(mine, 'tp', [(i, i ^ 1) for i in range(parts)])]
    dot_general x1 -> x0, local copies, waits for them, and re-layouts: 6.46 us -> none  [local(): kv_pairs = jnp.dot(normed, flat_weight, preferred_element_type=jnp.float32)]
  transfers between devices with their start and end apart: 2 -> 3, of which waited for: 2 -> 2; matrix products, arithmetic and copies ran while one was open for 8% -> 20% of each run, Pallas kernels for 0% -> 0%
where the time goes in v1:
time: 82.9 us; the launch traced here: 82.2 us
  starting transfers between devices  28.6 us (34%)
  waiting for transfers between devices  19.5 us (24%)
  local copies, waits for them, and re-layouts  19.4 us (23%)
  matrix products  7.54 us (9%)
  other arithmetic  6.36 us (8%)
  between operations  0.85 us (1%)
    all_to_all x2, starting transfers between devices, spread(): lax.all_to_all(jnp.broadcast_to(x[None], (count,) + x.shape), axis, 0, 0,...  19.7 us
    all_to_all x2, waiting for transfers between devices, spread(): lax.all_to_all(jnp.broadcast_to(x[None], (count,) + x.shape), axis, 0, 0,...  19.5 us
    another operation x2, local copies, waits for them, and re-layouts, local(): weight = w_kv[0].reshape(parts, D // parts, 2 * kv_local)  14.4 us
    ppermute x1, starting transfers between devices, local(): other = lax.ppermute(mine, 'tp', [(i, i ^ 1) for i in range(parts)])  8.89 us
    dot_general x1, matrix products, local(): jnp.einsum('prd,pdk->rk', normed, weight, preferred_element_type=jnp.floa...  4.57 us
    unnamed x12, local copies, waits for them, and re-layouts  2.73 us
  transfers between devices with their start and end apart: 3, of which 2 were waited for; matrix products, arithmetic and copies ran while one was open for 20% of the time, Pallas kernels for 0%

profile of v1, /device:TPU:1, one launch (start us, length us, event | category | flops | bytes accessed | tf_op | source)
XLA Modules:
  0.0 82.2 jit_solution(5508562420378507603)
XLA Ops:
  0.7 1.0 %convert_reduce_fusion = s32[4,16]{1,0:T(4,128)S(1)} fusion(s32[4,16]{1,0:T(4,128)} %param.12, pred[16,16]{1,0:T(8,128)(4,1)S(1)} %iota_compare_fusion.5), kind=kLoop, calls=%fused_computation.52 | loop fusion | flops 4032 | bytes 768 | tf_op jit(solution)/shard_map/reduce_sum | solution.py:40
  1.8 0.7 compare_convert_fusion
  2.6 1.0 %convolution_convert_fusion.1 = bf16[8,1024]{1,0:T(8,128)(2,1)S(1)} fusion(bf16[64,1024]{1,0:T(8,128)(2,1)} %bitcast.119, s32[64]{0:T(128)S(1)} %add.71, pred[64]{0:T(512)(128)(4,1)S(1)} %eq.147), kind=kOutput, calls=%fused_computation.18 | convolution fusion | flops 1057792 | bytes 147776 | tf_op jit(solution)/shard_map/dot_general | solution.py:48
  3.6 0.7 broadcast_in_dim.126
  4.3 15.7 %all-to-all-start = ((bf16[16,8,1024]{2,1,0:T(8,128)(2,1)}), bf16[16,8,1024]{2,1,0:T(8,128)(2,1)S(1)}, u32[]{:S(2)}, u32[]{:S(2)}) async-start(bf16[16,8,1024]{2,1,0:T(8,128)(2,1)} %broadcast_in_dim.126), calls=%async_computation | async-start | bytes 524288 | tf_op jit(solution)/shard_map/all_to_all | solution.py:30
  20.2 0.7 broadcast_multiply_fusion
  20.9 0.7 reduce.2
  21.7 12.2 %all-to-all-done = bf16[16,8,1024]{2,1,0:T(8,128)(2,1)S(1)} async-done(((bf16[16,8,1024]{2,1,0:T(8,128)(2,1)}), bf16[16,8,1024]{2,1,0:T(8,128)(2,1)S(1)}, u32[]{:S(2)}, u32[]{:S(2)}) %all-to-all-start) | async-done | bytes 262176 | tf_op jit(solution)/shard_map/all_to_all | solution.py:30
  33.9 1.1 %fusion.10 = bf16[64,1024]{1,0:T(8,128)(2,1)S(1)} fusion(bf16[64,1024]{1,0:T(8,128)(2,1)} %bitcast.120, bf16[16,8,1024]{2,1,0:T(8,128)(2,1)S(1)} %all-to-all-done, pred[64]{0:T(512)(128)(4,1)S(1)} %lt.44, s32[64]{0:T(128)S(1)} %add.72), kind=kOutput, calls=%fused_computation.16 | convolution fusion | flops 16924672 | bytes 524608 | tf_op jit(solution)/shard_map/dot_general | solution.py:55
  35.0 0.9 %broadcast_in_dim.129 = bf16[4,72,1024]{2,1,0:T(8,128)(2,1)} broadcast(bf16[72,1024]{1,0:T(8,128)(2,1)S(1)} %pad_maximum_fusion.1), dimensions={1,2} | broadcast | bytes 737280 | tf_op jit(solution)/shard_map/broadcast_in_dim | solution.py:31
  35.9 4.0 %all-to-all-start.1 = ((bf16[4,72,1024]{2,1,0:T(8,128)(2,1)}), bf16[4,72,1024]{2,1,0:T(8,128)(2,1)S(1)}, u32[]{:S(2)}, u32[]{:S(2)}) async-start(bf16[4,72,1024]{2,1,0:T(8,128)(2,1)} %broadcast_in_dim.129), calls=%async_computation.1 | async-start | bytes 1179648 | tf_op jit(solution)/shard_map/all_to_all | solution.py:30
  39.9 7.3 %all-to-all-done.1 = bf16[4,72,1024]{2,1,0:T(8,128)(2,1)S(1)} async-done(((bf16[4,72,1024]{2,1,0:T(8,128)(2,1)}), bf16[4,72,1024]{2,1,0:T(8,128)(2,1)S(1)}, u32[]{:S(2)}, u32[]{:S(2)}) %all-to-all-start.1) | async-done | bytes 589856 | tf_op jit(solution)/shard_map/all_to_all | solution.py:30
  47.2 8.9 %collective-permute-start = (bf16[4,72,1024]{2,1,0:T(8,128)(2,1)S(1)}, bf16[4,72,1024]{2,1,0:T(8,128)(2,1)S(1)}, u32[]{:S(2)}, u32[]{:S(2)}) collective-permute-start(bf16[4,72,1024]{2,1,0:T(8,128)(2,1)S(1)} %all-to-all-done.1), channel_id=1, source_target_pairs={{0,1},{1,0},{2,3},{3,2},{4,5},{5,4},{6,7},{7,6},{8,9},{9,8},{10,11... | collective-permute-start | bytes 1769480 | tf_op jit(solution)/shard_map/ppermute | solution.py:74
  56.3 7.6 %reshape.362 = bf16[8,1024,256]{2,1,0:T(8,128)(2,1)} reshape(bf16[1,8192,2,128]{3,2,1,0:T(2,128)(2,1)} %param.9) | data formatting | bytes 8388608 | tf_op jit(solution)/shard_map/reshape;squeeze | solution.py:84
  63.8 6.9 %copy.51 = bf16[8,1024,256]{1,0,2:T(8,128)(2,1)} copy(bf16[8,1024,256]{2,1,0:T(8,128)(2,1)} %reshape.362) | data formatting | bytes 8388608 | tf_op jit(solution)/shard_map/reshape;squeeze | solution.py:84
  71.3 0.3 fusion.3
  71.6 0.3 fusion.5
  71.9 1.4 %copy-done = bf16[8,1024,256]{1,0,2:T(8,128)(2,1)S(1)} copy-done((bf16[8,1024,256]{1,0,2:T(8,128)(2,1)S(1)}, bf16[8,1024,256]{1,0,2:T(8,128)(2,1)}, u32[]{:S(2)}) %copy-start) | copy-done | bytes 4194328
  73.3 4.6 %fusion.11 = f32[4,16,2,1,128]{4,1,2,0,3:T(8,128)S(1)} fusion(bf16[2,128,1024,8]{2,3,1,0:T(8,128)(2,1)S(1)} %bitcast.117, bf16[4,16,1024,8,1]{2,1,0,3,4:T(8,128)(2,1)S(1)} %bitcast.118), kind=kOutput, calls=%fused_computation.17 | convolution fusion | flops 268435456 | bytes 5308416 | tf_op jit(solution)/shard_map/prd,pdk->rk/dot_general | solution.py:85
  78.3 1.4 %fusion.16 = bf16[16,2,128,128]{3,2,0,1:T(8,128)(2,1)S(1)} fusion(bf16[1,16,2,128,128]{4,3,2,1,0:T(8,128)(2,1)S(1)} %copy-done.1, pred[16,128]{1,0:T(8,128)(4,1)S(1)} %get-tuple-element.27, pred[16,128]{1,0:T(8,128)(4,1)S(1)} %get-tuple-element.28, pred[16,128]{1,0:T(8,128)(4,1)S(1)} %get-tuple-element.29, pred[16,128]{1,0:T(8,128)(4,1)S(1)} %get-tuple-element.30, ...), kind=kLoop, calls=%fused_computation.22 | loop fusion | flops 2097152 | bytes 2138112 | tf_op jit(solution)/shard_map/jit(_where)/select_n | solution.py:97
  79.7 0.5 fusion.42
  80.5 0.3 fusion.8
  80.9 0.7 copy.41
  81.6 0.6 copy.42
  (40 shorter events, 1.8 us)
Async XLA Ops:
  0.6 39.3 %copy-start.3 = (s32[16]{0:T(128)S(1)}, s32[16]{0:T(128)}, u32[]{:S(2)}) copy-start(s32[16]{0:T(128)} %param.13) | copy-start | bytes 196
  4.3 29.5 %all-to-all-start = ((bf16[16,8,1024]{2,1,0:T(8,128)(2,1)}), bf16[16,8,1024]{2,1,0:T(8,128)(2,1)S(1)}, u32[]{:S(2)}, u32[]{:S(2)}) async-start(bf16[16,8,1024]{2,1,0:T(8,128)(2,1)} %broadcast_in_dim.126), calls=%async_computation | async-start | bytes 524288 | tf_op jit(solution)/shard_map/all_to_all | solution.py:30
  35.9 11.3 %all-to-all-start.1 = ((bf16[4,72,1024]{2,1,0:T(8,128)(2,1)}), bf16[4,72,1024]{2,1,0:T(8,128)(2,1)S(1)}, u32[]{:S(2)}, u32[]{:S(2)}) async-start(bf16[4,72,1024]{2,1,0:T(8,128)(2,1)} %broadcast_in_dim.129), calls=%async_computation.1 | async-start | bytes 1179648 | tf_op jit(solution)/shard_map/all_to_all | solution.py:30
  47.2 23.8 %collective-permute-start = (bf16[4,72,1024]{2,1,0:T(8,128)(2,1)S(1)}, bf16[4,72,1024]{2,1,0:T(8,128)(2,1)S(1)}, u32[]{:S(2)}, u32[]{:S(2)}) collective-permute-start(bf16[4,72,1024]{2,1,0:T(8,128)(2,1)S(1)} %all-to-all-done.1), channel_id=1, source_target_pairs={{0,1},{1,0},{2,3},{3,2},{4,5},{5,4},{6,7},{7,6},{8,9},{9,8},{10,11... | collective-permute-start | bytes 1769480 | tf_op jit(solution)/shard_map/ppermute | solution.py:74
  63.8 7.0 %copy-start.2 = (bf16[4,1,16,1024]{3,2,1,0:T(8,128)(2,1)S(1)}, bf16[4,1,16,1024]{3,2,1,0:T(8,128)(2,1)}, u32[]{:S(2)}) copy-start(bf16[4,1,16,1024]{3,2,1,0:T(8,128)(2,1)} %param.10) | copy-start | bytes 393220
  71.1 2.2 %copy-start = (bf16[8,1024,256]{1,0,2:T(8,128)(2,1)S(1)}, bf16[8,1024,256]{1,0,2:T(8,128)(2,1)}, u32[]{:S(2)}) copy-start(bf16[8,1024,256]{1,0,2:T(8,128)(2,1)} %copy.51) | copy-start | bytes 12582916
  73.3 5.0 %copy-start.1 = (bf16[1,16,2,128,128]{4,3,2,1,0:T(8,128)(2,1)S(1)}, bf16[1,16,2,128,128]{4,3,2,1,0:T(8,128)(2,1)}, u32[]{:S(2)}) copy-start(bf16[1,16,2,128,128]{4,3,2,1,0:T(8,128)(2,1)} %param.11) | copy-start | bytes 3145732

commit v2 on v0

v2 whole, which is shorter than its diff:
```python
import jax
import jax.numpy as jnp
from jax import lax
from jax.experimental import pallas as pl
from jax.experimental.pallas import tpu as pltpu
from jax.sharding import PartitionSpec as P

D = 8192
HEAD = 128
EXIT_CAP = 2
GAIN_ROWS = 8


EPSILON = 1e-05
ROPE_BASE = 500000.0
VMEM = pl.BlockSpec(memory_space=pltpu.VMEM)
SMEM = pl.BlockSpec(memory_space=pltpu.SMEM)


def iota(shape, axis):
    return lax.broadcasted_iota(jnp.int32, shape, axis)


def contract_last(a, b):
    return lax.dot_general(a, b, (((1,), (1,)), ((), ())), preferred_element_type=jnp.float32)


def leaving_kernel(reqs, section, exits_row, exits_column, own, out):
    rows = own.shape[0]
    slots = out.shape[1]
    by_row, by_column = exits_row[...], exits_column[...]
    first, second = iota((rows, rows), 0), iota((rows, rows), 1)
    earlier = (by_row == by_column) & (first < second) & (first // reqs == second // reqs)
    rank = jnp.sum(earlier.astype(jnp.float32), axis=0, keepdims=True).astype(jnp.int32)
    place = (iota((1, rows), 1) // reqs) * EXIT_CAP + rank
    pick = (iota((slots, rows), 0) == place) & (by_row == section[0])
    chosen = jnp.dot(
        pick.astype(jnp.float32).astype(jnp.bfloat16), own[...], preferred_element_type=jnp.float32
    ).astype(jnp.bfloat16)
    for k in range(out.shape[0]):
        out[k] = chosen


def ready_kernel(scale, lengths, weight, queries, cache, out_weight, out_old):
    step = pl.program_id(0)
    half = 128
    to, fro = iota((2 * half, 2 * half), 0), iota((2 * half, 2 * half), 1)
    split = (fro == jnp.where(to < half, 2 * to, 2 * (to - half) + 1)).astype(jnp.float32)
    split = split.astype(jnp.bfloat16)
    for j in range(weight.shape[0] // (2 * half)):
        pair = jnp.dot(
            split, weight[2 * half * j : 2 * half * (j + 1), :], preferred_element_type=jnp.float32
        ).astype(jnp.bfloat16)
        out_weight[0, half * j : half * (j + 1), 0:HEAD] = pair[:half]
        out_weight[0, half * j : half * (j + 1), HEAD : 2 * HEAD] = pair[half:]
    here = cache.shape[0]
    per = queries.shape[0] // here
    for k in range(here):
        length = lengths[step * here + k]
        span = slice(k * per, (k + 1) * per)
        scores = contract_last(queries[span, :], cache[k, 0]) * scale
        scores = jnp.where(iota(scores.shape, 1) < length, scores, -1e30)
        top = jnp.max(scores, axis=-1, keepdims=True)
        grown = jnp.exp(scores - top)
        total = jnp.sum(grown, axis=-1, keepdims=True)
        high = grown.astype(jnp.bfloat16)
        low = (grown - high.astype(jnp.float32)).astype(jnp.bfloat16)
        values = cache[k, 1]
        out_old[span, 0:HEAD] = jnp.dot(
            high, values, preferred_element_type=jnp.float32
        ) + jnp.dot(low, values, preferred_element_type=jnp.float32)
        out_old[span, HEAD : 2 * HEAD] = jnp.broadcast_to(top, (per, HEAD))
        out_old[span, 2 * HEAD : 3 * HEAD] = jnp.broadcast_to(total, (per, HEAD))


def place_kernel(take, kept, arrived, gain, out):
    rows = kept.shape[0]
    source = jnp.dot(take[...], arrived[...], preferred_element_type=jnp.float32)
    source = (source + kept[...].astype(jnp.float32)).astype(jnp.bfloat16)
    gains = jnp.broadcast_to(gain[...], (GAIN_ROWS, gain.shape[1]))
    for k in range(out.shape[0]):
        out[k, 0:rows, :] = source
        out[k, rows : rows + GAIN_ROWS, :] = gains


def finish_kernel(reqs, scale, core, mine, other, weight, queries, old, table, out_attn, out_kv):
    rows = queries.shape[0]
    chips = mine.shape[0]
    width = mine.shape[2]
    squares = jnp.zeros((rows, HEAD), jnp.float32)
    for held in (mine, other):
        for x in range(chips):
            for j in range(width // HEAD):
                value = held[x, 0:rows, HEAD * j : HEAD * (j + 1)].astype(jnp.float32)
                squares = squares + value * value
    mean = jnp.sum(squares, axis=-1, keepdims=True) / D
    inverse = lax.rsqrt(mean + EPSILON)
    pairs = jnp.zeros((rows, 2 * HEAD), jnp.float32)
    for held, parity in ((mine, core[0]), (other, 1 - core[0])):
        for x in range(chips):
            value = held[x, 0:rows, :].astype(jnp.float32)
            gain = held[x, rows : rows + 1, :].astype(jnp.float32)
            normed = (value * inverse * gain).astype(jnp.bfloat16)
            pairs = pairs + jnp.dot(
                normed, weight[2 * x + parity], preferred_element_type=jnp.float32
            )
    keys = pairs[:, :HEAD]
    turned = pltpu.roll(keys, HEAD // 2, 1)
    new_keys = (keys * table[0] + turned * table[1]).astype(jnp.bfloat16)
    new_values = pairs[:, HEAD:].astype(jnp.bfloat16)
    to, fro = iota((2 * rows, 2 * rows), 0), iota((2 * rows, 2 * rows), 1)
    weave = (fro == (to // 2) + rows * (to % 2)).astype(jnp.float32).astype(jnp.bfloat16)
    stacked = jnp.concatenate([new_keys, new_values], axis=0)
    out_kv[...] = jnp.dot(weave, stacked, preferred_element_type=jnp.float32).astype(jnp.bfloat16)
    by, of = iota((rows, rows), 0), iota((rows, rows), 1)
    seen = (by % reqs == of % reqs) & (of // reqs <= by // reqs)
    live = table[2]
    for g in range(old.shape[0]):
        span = slice(g * HEAD, (g + 1) * HEAD)
        scores = contract_last(queries[:, span], new_keys) * scale
        scores = jnp.where(seen, scores, -1e30)
        before, old_top, old_total = old[g, :, 0:HEAD], old[g, :, HEAD : HEAD + 1], old[g, :, 2 * HEAD : 2 * HEAD + 1]
        top = jnp.maximum(old_top, jnp.max(scores, axis=-1, keepdims=True))
        shrink = jnp.exp(old_top - top)
        grown = jnp.exp(scores - top)
        total = shrink * old_total + jnp.sum(grown, axis=-1, keepdims=True)
        fresh = (grown / total).astype(jnp.bfloat16)
        mixed = before * (shrink / total) + jnp.dot(
            fresh, new_values, preferred_element_type=jnp.float32
        )
        out_attn[:, span] = (mixed * live).astype(jnp.bfloat16)


def spread(x, axis, groups=None):
    return lax.all_to_all(x, axis, 0, 0, axis_index_groups=groups)


def local(hidden, norm_gain, w_kv, queries, cache_kv, exits, lengths):
    num_steps, _, local_reqs, width = hidden.shape
    rows = num_steps * local_reqs
    slots = num_steps * EXIT_CAP
    sections = lax.axis_size("section")
    section_index = lax.axis_index("section")
    parts = lax.axis_size("tp")
    chips = parts // 2
    core = lax.axis_index("tp") % 2
    kv_local = w_kv.shape[-1]
    cache_len = cache_kv.shape[3]
    groups = queries.shape[-1] // kv_local
    scale = HEAD ** (-0.5)

    own = hidden.reshape(rows, width)
    flat_exits = exits.reshape(rows)
    outgoing = pl.pallas_call(
        lambda *refs: leaving_kernel(local_reqs, *refs),
        out_shape=jax.ShapeDtypeStruct((sections, slots, width), jnp.bfloat16),
        in_specs=[SMEM, VMEM, VMEM, VMEM],
        out_specs=VMEM,
        name="leaving",
    )(section_index.reshape(1), flat_exits[None, :], flat_exits[:, None], own)
    arrived = spread(outgoing, "section").reshape(sections * slots, width)

    same = exits[:, :, None] == exits[:, None, :]
    earlier = jnp.arange(local_reqs)[None, None, :] < jnp.arange(local_reqs)[None, :, None]
    rank = jnp.sum((same & earlier).astype(jnp.int32), axis=-1)
    step_of = jnp.arange(num_steps, dtype=jnp.int32)[:, None]
    place = (step_of * EXIT_CAP + rank).reshape(rows)
    gone = flat_exits < section_index
    all_ids = jnp.arange(sections * slots, dtype=jnp.int32)
    take = (all_ids[None, :] == (flat_exits * slots + place)[:, None]) & gone[:, None]
    take = take.astype(jnp.bfloat16)
    kept = jnp.where(gone[:, None], jnp.zeros_like(own), own)
    positions = (lengths[None, :] + step_of).reshape(rows)
    exponent = jnp.arange(HEAD // 2, dtype=jnp.float32) * (2.0 / HEAD)
    angles = positions.astype(jnp.float32)[:, None] * ROPE_BASE ** (-exponent)
    cosine, sine = jnp.cos(angles), jnp.sin(angles)
    live = (section_index < flat_exits).astype(jnp.float32)
    table = jnp.stack(
        [
            jnp.concatenate([cosine, cosine], axis=-1),
            jnp.concatenate([-sine, sine], axis=-1),
            jnp.broadcast_to(live[:, None], (rows, HEAD)),
        ]
    )
    by_request = queries.reshape(num_steps, local_reqs, groups, HEAD).transpose(1, 0, 2, 3)
    here = local_reqs // parts
    weight, old = pl.pallas_call(
        lambda *refs: ready_kernel(scale, *refs),
        grid=(parts,),
        out_shape=(
            jax.ShapeDtypeStruct((parts, width, 2 * HEAD), jnp.bfloat16),
            jax.ShapeDtypeStruct((rows * groups, 3 * HEAD), jnp.float32),
        ),
        in_specs=[
            SMEM,
            pl.BlockSpec((2 * width, HEAD), lambda i: (i, 0)),
            pl.BlockSpec((here * num_steps * groups, HEAD), lambda i: (i, 0)),
            pl.BlockSpec((here, 2, cache_len, HEAD), lambda i: (i, 0, 0, 0)),
        ],
        out_specs=(
            pl.BlockSpec((1, width, 2 * HEAD), lambda i: (i, 0, 0)),
            pl.BlockSpec((here * num_steps * groups, 3 * HEAD), lambda i: (i, 0)),
        ),
        name="ready",
    )(
        lengths,
        w_kv.reshape(2 * D, HEAD),
        by_request.reshape(rows * groups, HEAD),
        cache_kv[0],
    )
    old = old.reshape(local_reqs, num_steps, groups, 3 * HEAD).transpose(2, 1, 0, 3)
    old = old.reshape(groups, rows, 3 * HEAD)

    weight, old, table, take, kept, arrived = lax.optimization_barrier(
        (weight, old, table, take, kept, arrived)
    )
    sent = pl.pallas_call(
        place_kernel,
        out_shape=jax.ShapeDtypeStruct((chips, rows + GAIN_ROWS, width), jnp.bfloat16),
        in_specs=[VMEM] * 4,
        out_specs=VMEM,
        name="place",
    )(take, kept, arrived, norm_gain)
    same_core = [[2 * x + c for x in range(chips)] for c in range(2)]
    mine = spread(sent, "tp", same_core)
    other = lax.ppermute(mine, "tp", [(i, i ^ 1) for i in range(parts)])

    attended, fresh = pl.pallas_call(
        lambda *refs: finish_kernel(local_reqs, scale, *refs),
        out_shape=(
            jax.ShapeDtypeStruct((rows, groups * HEAD), jnp.bfloat16),
            jax.ShapeDtypeStruct((2 * rows, HEAD), jnp.bfloat16),
        ),
        in_specs=[SMEM] + [VMEM] * 6,
        out_specs=(VMEM, VMEM),
        name="finish",
    )(core.reshape(1), mine, other, weight, queries.reshape(rows, groups * HEAD), old, table)
    return (
        attended.reshape(num_steps, 1, local_reqs, groups * HEAD),
        fresh.reshape(num_steps, 1, local_reqs, 2, kv_local),
    )


def solution(mesh):
    placed = (
        P(None, "section", "req", "tp"),
        P("section", "tp"),
        P("section", None, None, "tp"),
        P(None, "section", "req", "tp"),
        P("section", "req", None, None, "tp"),
        P(None, "req"),
        P("req"),
    )
    return jax.shard_map(
        local,
        mesh=mesh,
        in_specs=placed,
        out_specs=(P(None, "section", "req", "tp"), P(None, "section", "req", None, "tp")),
        check_vma=False,
    )
```

time: 162 us -> 71.2 us (0.44)
  waiting for transfers between devices: 83.8 us -> 1.6 us
  Pallas kernels: 0 us -> 21.1 us
  starting transfers between devices: 0.08 us -> 20 us
  other arithmetic: 23.4 us -> 5.45 us
  between operations: 14.1 us -> 0.71 us
  blocking collectives: 21.6 us -> 12.9 us
  matrix products: 4.78 us -> 0 us
  local copies, waits for them, and re-layouts: 12.8 us -> 8.74 us
    all_gather x2 -> x0, waiting for transfers between devices: 83.7 us -> none  [the longest x1 69.1 us: carried_in(): everything = lax.all_gather(x, axis)]
    psum x1 -> x0, blocking collectives: 21.6 us -> none  [local(): squares = lax.psum(jnp.sum(rows_float * rows_float, axis=-1), 'tp')]
    pallas_call x0 -> x4, Pallas kernels: none -> 21.1 us  [the longest x1 8.88 us: local(): pl.pallas_call(lambda *refs: ready_kernel(scale, *refs), grid=(parts,), o...]
    select_n x18 -> x1, other arithmetic: 18.3 us -> 0.74 us  [local(): kept = jnp.where(gone[:, None], jnp.zeros_like(own), own)]
    all_to_all x0 -> x1, starting transfers between devices: none -> 15.9 us  [spread(): return lax.all_to_all(x, axis, 0, 0, axis_index_groups=groups)]
    all_to_all x0 -> x1, blocking collectives: none -> 12.9 us  [spread(): return lax.all_to_all(x, axis, 0, 0, axis_index_groups=groups)]
    dot_general x1 -> x0, local copies, waits for them, and re-layouts: 6.46 us -> none  [local(): kv_pairs = jnp.dot(normed, flat_weight, preferred_element_type=jnp.float32)]
    dot_general x3 -> x0, matrix products: 4.78 us -> none  [the longest x1 3.98 us: local(): kv_pairs = jnp.dot(normed, flat_weight, preferred_element_type=jnp.float32)]
  transfers between devices with their start and end apart: 2 -> 2, of which waited for: 2 -> 1; matrix products, arithmetic and copies ran while one was open for 8% -> 14% of each run, Pallas kernels for 0% -> 13%
where the time goes in v2:
time: 71.2 us; the launch traced here: 70.5 us
  Pallas kernels  21.1 us (30%)
  starting transfers between devices  20 us (28%)
  blocking collectives  12.9 us (18%)
  local copies, waits for them, and re-layouts  8.74 us (12%)
  other arithmetic  5.45 us (8%)
  waiting for transfers between devices  1.6 us (2%)
    all_to_all x1, starting transfers between devices, spread(): return lax.all_to_all(x, axis, 0, 0, axis_index_groups=groups)  15.9 us
    all_to_all x1, blocking collectives, spread(): return lax.all_to_all(x, axis, 0, 0, axis_index_groups=groups)  12.9 us
    pallas_call x1, Pallas kernels, local(): pl.pallas_call(lambda *refs: ready_kernel(scale, *refs), grid=(parts,), o...  8.88 us
    pallas_call x1, Pallas kernels, local(): pl.pallas_call(lambda *refs: finish_kernel(local_reqs, scale, *refs), out...  8.35 us
    ppermute x1, starting transfers between devices, local(): other = lax.ppermute(mine, 'tp', [(i, i ^ 1) for i in range(parts)])  4.11 us
    reshape x1, local copies, waits for them, and re-layouts, local(): old.reshape(local_reqs, num_steps, groups, 3 * HEAD).transpose(2, 1, 0, 3)  2.48 us
    unnamed x9, local copies, waits for them, and re-layouts  2.46 us
    pallas_call x1, Pallas kernels, local(): pl.pallas_call(place_kernel, out_shape=jax.ShapeDtypeStruct((chips, rows...  2.05 us
  transfers between devices with their start and end apart: 2, of which 1 were waited for; matrix products, arithmetic and copies ran while one was open for 14% of the time, Pallas kernels for 13%

profile of v2, /device:TPU:1, one launch (start us, length us, event | category | flops | bytes accessed | tf_op | source)
XLA Modules:
  0.0 70.5 jit_solution(16389424622196433258)
XLA Ops:
  0.6 1.3 %broadcast_in_dim_reshape.4.refs_1_ = s32[1,64]{1,0:T(1,128)} reshape(s32[4,16]{1,0:T(4,128)} %param.12) | data formatting | bytes 512 | tf_op jit(solution)/shard_map/broadcast_in_dim;reshape | solution.py:160
  2.0 1.4 %reshape.134.refs_2_ = s32[64,1]{1,0:T(8,128)} reshape(s32[4,16]{1,0:T(4,128)} %param.12) | data formatting | bytes 512 | tf_op jit(solution)/shard_map/reshape | solution.py:153
  3.3 1.9 %leaving.1 = bf16[16,8,1024]{2,1,0:T(8,128)(2,1)} custom-call(s32[1]{0:T(128)} %bitcast.11.refs_0_, s32[1,64]{1,0:T(1,128)} %broadcast_in_dim_reshape.4.refs_1_, s32[64,1]{1,0:T(8,128)} %reshape.134.refs_2_, bf16[64,1024]{1,0:T(8,128)(2,1)} %bitcast.38), custom_call_target="tpu_custom_call" | custom-call | tf_op jit(solution)/shard_map/leaving/pallas_call | solution.py:154
  5.2 15.9 %all-to-all-start = ((bf16[16,8,1024]{2,1,0:T(8,128)(2,1)}), bf16[16,8,1024]{2,1,0:T(8,128)(2,1)S(1)}, u32[]{:S(2)}, u32[]{:S(2)}) async-start(bf16[16,8,1024]{2,1,0:T(8,128)(2,1)} %leaving.1), calls=%async_computation | async-start | bytes 524288 | tf_op jit(solution)/shard_map/all_to_all | solution.py:135
  21.1 0.7 broadcast_compare_fusion
  21.8 0.7 add_convert_fusion
  22.5 1.0 %convert_reduce_fusion = s32[4,16]{1,0:T(4,128)S(1)} fusion(s32[4,16]{1,0:T(4,128)} %param.12, pred[16,16]{1,0:T(8,128)(4,1)S(1)} %iota_compare_fusion.1), kind=kLoop, calls=%fused_computation.6 | loop fusion | flops 4032 | bytes 768 | tf_op jit(solution)/shard_map/reduce_sum | solution.py:165
  23.5 0.8 %add_add_fusion = s32[4,16]{1,0:T(4,128)S(1)} fusion(s32[4,16]{1,0:T(4,128)S(1)} %convert_reduce_fusion, s32[4,16]{1,0:T(4,128)} %param.12, s32[4]{0:T(128)S(1)} %iota_multiply_fusion), kind=kLoop, calls=%fused_computation.12 | loop fusion | flops 192 | bytes 784 | tf_op jit(solution)/shard_map/add | solution.py:170
  24.4 0.1 lt.49
  24.5 0.9 %copy.19 = bf16[8,8,8,128]{3,2,1,0:T(8,128)(2,1)S(1)} copy(bf16[8,8,8,128]{3,1,2,0:T(8,128)(2,1)} %bitcast.35) | data formatting | bytes 262144
  25.5 0.7 copy.14
  26.1 8.9 %ready.1 = (bf16[8,1024,256]{2,1,0:T(8,128)(2,1)}, f32[512,384]{1,0:T(8,128)}) custom-call(s32[16]{0:T(128)} %refs_0_.1, bf16[16384,128]{1,0:T(8,128)(2,1)} %bitcast.30, bf16[512,128]{1,0:T(8,128)(2,1)} %bitcast.37, bf16[16,2,128,128]{3,2,1,0:T(8,128)(2,1)} %bitcast.33), custom_call_target="tpu_custom_call" | custom-call | tf_op jit(solution)/shard_map/ready/pallas_call | solution.py:187
  35.0 2.5 %copy.15 = f32[16,4,8,384]{3,0,1,2:T(8,128)} copy(f32[16,4,8,384]{3,2,1,0:T(8,128)} %bitcast.34) | data formatting | bytes 1572864 | tf_op jit(solution)/shard_map/reshape | solution.py:211
  37.5 0.2 multiply_cosine_fusion
  37.9 0.6 pad_maximum_fusion.refs_6_
  38.5 0.7 fusion.1.take
  39.2 0.7 %broadcast_select_fusion.kept = bf16[64,1024]{1,0:T(8,128)(2,1)} fusion(pred[64]{0:T(512)(128)(4,1)S(1)} %lt.49, bf16[4,1,16,1024]{3,2,1,0:T(8,128)(2,1)S(1)} %copy-done.3), kind=kLoop, calls=%fused_computation | loop fusion | flops 65536 | bytes 262208 | tf_op jit(solution)/shard_map/jit(_where)/select_n | solution.py:172
  40.0 0.7 %copy-done.1 = bf16[16,8,1024]{2,1,0:T(8,128)(2,1)} copy-done((bf16[16,8,1024]{2,1,0:T(8,128)(2,1)}, bf16[16,8,1024]{2,1,0:T(8,128)(2,1)S(1)}, u32[]{:S(2)}) %copy-start.1) | copy-done | bytes 262168
  40.7 2.0 %place.1 = bf16[4,72,1024]{2,1,0:T(8,128)(2,1)} custom-call(bf16[64,128]{1,0:T(8,128)(2,1)} %fusion.1.take, bf16[64,1024]{1,0:T(8,128)(2,1)} %broadcast_select_fusion.kept, bf16[128,1024]{1,0:T(8,128)(2,1)} %bitcast.32, bf16[1,1024]{1,0:T(2,128)(2,1)} %gain.1), custom_call_target="tpu_custom_call" | custom-call | tf_op jit(solution)/shard_map/place/pallas_call | solution.py:217
  42.7 12.9 %all_to_all.10.refs_1_ = bf16[4,72,1024]{2,1,0:T(8,128)(2,1)S(1)} all-to-all(bf16[4,72,1024]{2,1,0:T(8,128)(2,1)} %place.1), channel_id=1, replica_groups={{0,2,4,6},{1,3,5,7},{8,10,12,14},{9,11,13,15},{16,18,20,22},{17,19,21,2..., dimensions={0} | all-to-all | bytes 1179648 | tf_op jit(solution)/shard_map/all_to_all | solution.py:135
  55.6 4.1 %collective-permute-start = (bf16[4,72,1024]{2,1,0:T(8,128)(2,1)S(1)}, bf16[4,72,1024]{2,1,0:T(8,128)(2,1)S(1)}, u32[]{:S(2)}, u32[]{:S(2)}) collective-permute-start(bf16[4,72,1024]{2,1,0:T(8,128)(2,1)S(1)} %all_to_all.10.refs_1_), channel_id=1, source_target_pairs={{0,1},{1,0},{2,3},{3,2},{4,5},{5,4},{6,7},{7,6},{8,9},{9,8},{10,11... | collective-permute-start | bytes 1769480 | tf_op jit(solution)/shard_map/ppermute | solution.py:226
  59.8 1.6 %collective-permute-done.refs_2_ = bf16[4,72,1024]{2,1,0:T(8,128)(2,1)S(1)} collective-permute-done((bf16[4,72,1024]{2,1,0:T(8,128)(2,1)S(1)}, bf16[4,72,1024]{2,1,0:T(8,128)(2,1)S(1)}, u32[]{:S(2)}, u32[]{:S(2)}) %collective-permute-start) | collective-permute-done | bytes 589856 | tf_op jit(solution)/shard_map/ppermute | solution.py:226
  61.4 0.8 %copy-done.2 = bf16[4,72,1024]{2,1,0:T(8,128)(2,1)} copy-done((bf16[4,72,1024]{2,1,0:T(8,128)(2,1)}, bf16[4,72,1024]{2,1,0:T(8,128)(2,1)S(1)}, u32[]{:S(2)}) %copy-start.2) | copy-done | bytes 589848
  62.2 8.3 %finish.1 = (bf16[64,1024]{1,0:T(8,128)(2,1)}, bf16[128,128]{1,0:T(8,128)(2,1)}) custom-call(s32[1]{0:T(128)} %bitcast.refs_0_, bf16[4,72,1024]{2,1,0:T(8,128)(2,1)} %copy-done, bf16[4,72,1024]{2,1,0:T(8,128)(2,1)} %copy-done.2, bf16[8,1024,256]{2,1,0:T(8,128)(2,1)} %get-tuple-element.17.refs_3_, bf16[64,1024]{1,0:T(8,128)(2,1)} %bitcast.36, ...), custom_call_target="tpu_custom_call" | custom-call | tf_op jit(solution)/shard_map/finish/pallas_call | solution.py:228
  (15 shorter events, 0.4 us)
Async XLA Ops:
  5.2 34.0 %copy-start.3 = (bf16[4,1,16,1024]{3,2,1,0:T(8,128)(2,1)S(1)}, bf16[4,1,16,1024]{3,2,1,0:T(8,128)(2,1)}, u32[]{:S(2)}) copy-start(bf16[4,1,16,1024]{3,2,1,0:T(8,128)(2,1)} %param.7) | copy-start | bytes 393220
  5.2 34.7 %all-to-all-start = ((bf16[16,8,1024]{2,1,0:T(8,128)(2,1)}), bf16[16,8,1024]{2,1,0:T(8,128)(2,1)S(1)}, u32[]{:S(2)}, u32[]{:S(2)}) async-start(bf16[16,8,1024]{2,1,0:T(8,128)(2,1)} %leaving.1), calls=%async_computation | async-start | bytes 524288 | tf_op jit(solution)/shard_map/all_to_all | solution.py:135
  39.9 0.7 %copy-start.1 = (bf16[16,8,1024]{2,1,0:T(8,128)(2,1)}, bf16[16,8,1024]{2,1,0:T(8,128)(2,1)S(1)}, u32[]{:S(2)}) copy-start(bf16[16,8,1024]{2,1,0:T(8,128)(2,1)S(1)} %all-to-all-done) | copy-start | bytes 786436
  55.6 5.7 %copy-start = (bf16[4,72,1024]{2,1,0:T(8,128)(2,1)}, bf16[4,72,1024]{2,1,0:T(8,128)(2,1)S(1)}, u32[]{:S(2)}) copy-start(bf16[4,72,1024]{2,1,0:T(8,128)(2,1)S(1)} %all_to_all.10.refs_1_) | copy-start | bytes 1769476
  55.6 5.7 %collective-permute-start = (bf16[4,72,1024]{2,1,0:T(8,128)(2,1)S(1)}, bf16[4,72,1024]{2,1,0:T(8,128)(2,1)S(1)}, u32[]{:S(2)}, u32[]{:S(2)}) collective-permute-start(bf16[4,72,1024]{2,1,0:T(8,128)(2,1)S(1)} %all_to_all.10.refs_1_), channel_id=1, source_target_pairs={{0,1},{1,0},{2,3},{3,2},{4,5},{5,4},{6,7},{7,6},{8,9},{9,8},{10,11... | collective-permute-start | bytes 1769480 | tf_op jit(solution)/shard_map/ppermute | solution.py:226
  61.4 0.8 %copy-start.2 = (bf16[4,72,1024]{2,1,0:T(8,128)(2,1)}, bf16[4,72,1024]{2,1,0:T(8,128)(2,1)S(1)}, u32[]{:S(2)}) copy-start(bf16[4,72,1024]{2,1,0:T(8,128)(2,1)S(1)} %collective-permute-done.refs_2_) | copy-start | bytes 1769476

commit v3 on v2

v3 whole, which is shorter than its diff:
```python
import jax
import jax.numpy as jnp
from jax import lax
from jax.experimental import pallas as pl
from jax.experimental.pallas import tpu as pltpu
from jax.sharding import PartitionSpec as P

D = 8192
HEAD = 128
EXIT_CAP = 2
GAIN_ROWS = 8


EPSILON = 1e-05
ROPE_BASE = 500000.0
VMEM = pl.BlockSpec(memory_space=pltpu.VMEM)
SMEM = pl.BlockSpec(memory_space=pltpu.SMEM)


def iota(shape, axis):
    return lax.broadcasted_iota(jnp.int32, shape, axis)


def contract_last(a, b):
    return lax.dot_general(a, b, (((1,), (1,)), ((), ())), preferred_element_type=jnp.float32)


def as_bf16(mask):
    return mask.astype(jnp.float32).astype(jnp.bfloat16)


def exact(a, b):
    return jnp.dot(a, b, preferred_element_type=jnp.float32)


def ranks(same):
    reqs = same.shape[1]
    before = iota((reqs, reqs), 0) < iota((reqs, reqs), 1)
    return exact(as_bf16(same), as_bf16(before))


def leaving_kernel(section, exits, own, out):
    steps, reqs = exits.shape
    rows = own.shape[0]
    here = exits[...] == section[0]
    rank = ranks(here)
    picks = [here & (rank == k) for k in range(EXIT_CAP)]
    picks = jnp.concatenate([pick.astype(jnp.float32) for pick in picks], axis=0)
    widen = as_bf16(iota((reqs, rows), 0) == iota((reqs, rows), 1) % reqs)
    wide = exact(picks.astype(jnp.bfloat16), widen)
    slots = EXIT_CAP * steps
    match = iota((slots, rows), 0) % steps == iota((slots, rows), 1) // reqs
    wide = jnp.where(match, wide, 0.0).astype(jnp.bfloat16)
    chosen = exact(wide, own[...]).astype(jnp.bfloat16)
    for k in range(out.shape[0]):
        out[k] = chosen


def choose_kernel(section, exits, own, take, kept):
    steps, reqs = exits.shape
    rows, reach = take.shape
    slots = EXIT_CAP * steps
    layer = exits[...]
    rank = jnp.zeros((steps, reqs), jnp.float32)
    for e in range(reach // slots):
        same = layer == e
        rank = jnp.where(same, ranks(same), rank)
    gone = layer < section[0]
    slot = layer * slots + rank.astype(jnp.int32) * steps + iota((steps, reqs), 0)
    slot = jnp.where(gone, slot, -1).astype(jnp.float32)
    spread_steps = as_bf16(iota((rows, steps), 0) // reqs == iota((rows, steps), 1))
    column = exact(spread_steps, slot.astype(jnp.bfloat16))
    own_lane = iota((rows, reqs), 0) % reqs == iota((rows, reqs), 1)
    column = jnp.sum(jnp.where(own_lane, column, 0.0), axis=-1, keepdims=True)
    take[...] = as_bf16(column.astype(jnp.int32) == iota((rows, reach), 1))
    kept[...] = jnp.where(column >= 0.0, 0.0, own[...].astype(jnp.float32)).astype(jnp.bfloat16)


def split_kernel(weight, out):
    half = 128
    to, fro = iota((2 * half, 2 * half), 0), iota((2 * half, 2 * half), 1)
    split = as_bf16(fro == jnp.where(to < half, 2 * to, 2 * (to - half) + 1))
    for j in range(weight.shape[0] // (2 * half)):
        pair = exact(split, weight[2 * half * j : 2 * half * (j + 1), :]).astype(jnp.bfloat16)
        out[0, half * j : half * (j + 1), 0:HEAD] = pair[:half]
        out[0, half * j : half * (j + 1), HEAD : 2 * HEAD] = pair[half:]


def past_kernel(scale, lengths, queries, cache, out):
    reqs = cache.shape[0]
    per = queries.shape[0] // reqs
    groups = out.shape[0]
    for r in range(reqs):
        scores = contract_last(queries[r * per : (r + 1) * per, :], cache[r, 0]) * scale
        scores = jnp.where(iota(scores.shape, 1) < lengths[r], scores, -1e30)
        top = jnp.max(scores, axis=-1, keepdims=True)
        grown = jnp.exp(scores - top)
        total = jnp.sum(grown, axis=-1, keepdims=True)
        high = grown.astype(jnp.bfloat16)
        low = (grown - high.astype(jnp.float32)).astype(jnp.bfloat16)
        mixed = exact(high, cache[r, 1]) + exact(low, cache[r, 1])
        top = jnp.broadcast_to(top, (per, HEAD))
        total = jnp.broadcast_to(total, (per, HEAD))
        for t in range(per // groups):
            row = slice(t * reqs + r, t * reqs + r + 1)
            for g in range(groups):
                at = slice(t * groups + g, t * groups + g + 1)
                out[g, row, 0:HEAD] = mixed[at]
                out[g, row, HEAD : 2 * HEAD] = top[at]
                out[g, row, 2 * HEAD : 3 * HEAD] = total[at]


def place_kernel(take, kept, arrived, gain, out):
    rows = kept.shape[0]
    source = jnp.dot(take[...], arrived[...], preferred_element_type=jnp.float32)
    source = (source + kept[...].astype(jnp.float32)).astype(jnp.bfloat16)
    gains = jnp.broadcast_to(gain[...], (GAIN_ROWS, gain.shape[1]))
    for k in range(out.shape[0]):
        out[k, 0:rows, :] = source
        out[k, rows : rows + GAIN_ROWS, :] = gains


def finish_kernel(
    reqs, scale, core, mine, other, weight, queries, old, table, out_attn, out_kv, held_weight, sems
):
    rows = queries.shape[0]
    chips = mine.shape[0]
    width = mine.shape[2]
    order = [(mine, x, 2 * x + core[0]) for x in range(chips)]
    order += [(other, x, 2 * x + 1 - core[0]) for x in range(chips)]
    loads = [
        pltpu.make_async_copy(weight.at[part], held_weight.at[i], sems.at[i])
        for i, (_, _, part) in enumerate(order)
    ]
    for load in loads:
        load.start()
    squares = jnp.zeros((rows, HEAD), jnp.float32)
    for held in (mine, other):
        for x in range(chips):
            for j in range(width // HEAD):
                value = held[x, 0:rows, HEAD * j : HEAD * (j + 1)].astype(jnp.float32)
                squares = squares + value * value
    mean = jnp.sum(squares, axis=-1, keepdims=True) / D
    inverse = lax.rsqrt(mean + EPSILON)
    pairs = jnp.zeros((rows, 2 * HEAD), jnp.float32)
    for i, (held, x, _) in enumerate(order):
        value = held[x, 0:rows, :].astype(jnp.float32)
        gain = held[x, rows : rows + 1, :].astype(jnp.float32)
        normed = (value * inverse * gain).astype(jnp.bfloat16)
        loads[i].wait()
        pairs = pairs + exact(normed, held_weight[i])
    keys = pairs[:, :HEAD]
    turned = pltpu.roll(keys, HEAD // 2, 1)
    new_keys = (keys * table[0] + turned * table[1]).astype(jnp.bfloat16)
    new_values = pairs[:, HEAD:].astype(jnp.bfloat16)
    to, fro = iota((2 * rows, 2 * rows), 0), iota((2 * rows, 2 * rows), 1)
    weave = (fro == (to // 2) + rows * (to % 2)).astype(jnp.float32).astype(jnp.bfloat16)
    stacked = jnp.concatenate([new_keys, new_values], axis=0)
    out_kv[...] = jnp.dot(weave, stacked, preferred_element_type=jnp.float32).astype(jnp.bfloat16)
    by, of = iota((rows, rows), 0), iota((rows, rows), 1)
    seen = (by % reqs == of % reqs) & (of // reqs <= by // reqs)
    live = table[2]
    for g in range(old.shape[0]):
        span = slice(g * HEAD, (g + 1) * HEAD)
        scores = contract_last(queries[:, span], new_keys) * scale
        scores = jnp.where(seen, scores, -1e30)
        before, old_top, old_total = old[g, :, 0:HEAD], old[g, :, HEAD : HEAD + 1], old[g, :, 2 * HEAD : 2 * HEAD + 1]
        top = jnp.maximum(old_top, jnp.max(scores, axis=-1, keepdims=True))
        shrink = jnp.exp(old_top - top)
        grown = jnp.exp(scores - top)
        total = shrink * old_total + jnp.sum(grown, axis=-1, keepdims=True)
        fresh = (grown / total).astype(jnp.bfloat16)
        mixed = before * (shrink / total) + jnp.dot(
            fresh, new_values, preferred_element_type=jnp.float32
        )
        out_attn[:, span] = (mixed * live).astype(jnp.bfloat16)


def near(x):
    return pltpu.with_memory_space_constraint(x, pltpu.VMEM)


def small(mebibytes):
    return pltpu.CompilerParams(vmem_limit_bytes=mebibytes << 20)


def spread(x, axis, groups=None):
    return lax.all_to_all(x, axis, 0, 0, axis_index_groups=groups)


def local(hidden, norm_gain, w_kv, queries, cache_kv, exits, lengths):
    num_steps, _, local_reqs, width = hidden.shape
    rows = num_steps * local_reqs
    slots = num_steps * EXIT_CAP
    sections = lax.axis_size("section")
    section_index = lax.axis_index("section")
    parts = lax.axis_size("tp")
    chips = parts // 2
    core = lax.axis_index("tp") % 2
    kv_local = w_kv.shape[-1]
    groups = queries.shape[-1] // kv_local
    scale = HEAD ** (-0.5)

    own = hidden.reshape(rows, width)
    flat_exits = exits.reshape(rows)
    section_scalar = section_index.reshape(1)
    outgoing = pl.pallas_call(
        leaving_kernel,
        out_shape=pltpu.VMEM((sections, slots, width), jnp.bfloat16),
        in_specs=[SMEM, VMEM, VMEM],
        out_specs=VMEM,
        compiler_params=small(4),
        name="leaving",
    )(section_scalar, exits, own)
    arrived = spread(outgoing, "section").reshape(sections * slots, width)

    take, kept = pl.pallas_call(
        choose_kernel,
        out_shape=(
            pltpu.VMEM((rows, sections * slots), jnp.bfloat16),
            pltpu.VMEM((rows, width), jnp.bfloat16),
        ),
        in_specs=[SMEM, VMEM, VMEM],
        out_specs=(VMEM, VMEM),
        compiler_params=small(4),
        name="choose",
    )(section_scalar, exits, own)
    step_of = jnp.arange(num_steps, dtype=jnp.int32)[:, None]
    positions = (lengths[None, :] + step_of).reshape(rows)
    exponent = jnp.arange(HEAD // 2, dtype=jnp.float32) * (2.0 / HEAD)
    angles = positions.astype(jnp.float32)[:, None] * ROPE_BASE ** (-exponent)
    cosine, sine = jnp.cos(angles), jnp.sin(angles)
    live = (section_index < flat_exits).astype(jnp.float32)
    table = jnp.stack(
        [
            jnp.concatenate([cosine, cosine], axis=-1),
            jnp.concatenate([-sine, sine], axis=-1),
            jnp.broadcast_to(live[:, None], (rows, HEAD)),
        ]
    )
    by_request = queries.reshape(num_steps, local_reqs, groups, HEAD).transpose(1, 0, 2, 3)
    weight = pl.pallas_call(
        split_kernel,
        grid=(parts,),
        out_shape=pltpu.HBM((parts, width, 2 * HEAD), jnp.bfloat16),
        in_specs=[pl.BlockSpec((2 * width, HEAD), lambda i: (i, 0))],
        out_specs=pl.BlockSpec((1, width, 2 * HEAD), lambda i: (i, 0, 0)),
        compiler_params=small(8),
        name="split",
    )(pltpu.with_memory_space_constraint(w_kv.reshape(2 * D, HEAD), pltpu.HBM))
    old = pl.pallas_call(
        lambda *refs: past_kernel(scale, *refs),
        out_shape=pltpu.VMEM((groups, rows, 3 * HEAD), jnp.float32),
        in_specs=[SMEM, VMEM, VMEM],
        out_specs=VMEM,
        compiler_params=small(8),
        name="past",
    )(lengths, near(by_request.reshape(rows * groups, HEAD)), near(cache_kv[0]))

    weight, old, table, take, kept, arrived = lax.optimization_barrier(
        (weight, old, table, take, kept, arrived)
    )
    sent = pl.pallas_call(
        place_kernel,
        out_shape=pltpu.VMEM((chips, rows + GAIN_ROWS, width), jnp.bfloat16),
        in_specs=[VMEM] * 4,
        out_specs=VMEM,
        compiler_params=small(4),
        name="place",
    )(near(take), near(kept), near(arrived), near(norm_gain))
    same_core = [[2 * x + c for x in range(chips)] for c in range(2)]
    mine = spread(sent, "tp", same_core)
    other = lax.ppermute(mine, "tp", [(i, i ^ 1) for i in range(parts)])

    attended, fresh = pl.pallas_call(
        lambda *refs: finish_kernel(local_reqs, scale, *refs),
        out_shape=(
            jax.ShapeDtypeStruct((rows, groups * HEAD), jnp.bfloat16),
            jax.ShapeDtypeStruct((2 * rows, HEAD), jnp.bfloat16),
        ),
        in_specs=[SMEM, VMEM, VMEM, pl.BlockSpec(memory_space=pltpu.HBM)] + [VMEM] * 3,
        out_specs=(VMEM, VMEM),
        scratch_shapes=[
            pltpu.VMEM((parts, width, 2 * HEAD), jnp.bfloat16),
            pltpu.SemaphoreType.DMA((parts,)),
        ],
        compiler_params=small(24),
        name="finish",
    )(
        core.reshape(1),
        near(mine),
        near(other),
        pltpu.with_memory_space_constraint(weight, pltpu.HBM),
        near(queries.reshape(rows, groups * HEAD)),
        near(old),
        near(table),
    )
    return (
        attended.reshape(num_steps, 1, local_reqs, groups * HEAD),
        fresh.reshape(num_steps, 1, local_reqs, 2, kv_local),
    )


def solution(mesh):
    placed = (
        P(None, "section", "req", "tp"),
        P("section", "tp"),
        P("section", None, None, "tp"),
        P(None, "section", "req", "tp"),
        P("section", "req", None, None, "tp"),
        P(None, "req"),
        P("req"),
    )
    return jax.shard_map(
        local,
        mesh=mesh,
        in_specs=placed,
        out_specs=(P(None, "section", "req", "tp"), P(None, "section", "req", None, "tp")),
        check_vma=False,
    )
```

time: 71.2 us -> 62.3 us (0.87)
  local copies, waits for them, and re-layouts: 8.74 us -> 3.69 us
  starting transfers between devices: 20 us -> 24.6 us
  other arithmetic: 5.45 us -> 0.97 us
  Pallas kernels: 21.1 us -> 18.4 us
  blocking collectives: 12.9 us -> 11.1 us
    ppermute x1, starting transfers between devices: 4.11 us -> 8.89 us  [local(): other = lax.ppermute(mine, 'tp', [(i, i ^ 1) for i in range(parts)])]
    reshape x2 -> x0, local copies, waits for them, and re-layouts: 3.86 us -> none  [the longest x1 2.48 us: local(): old.reshape(local_reqs, num_steps, groups, 3 * HEAD).transpose(2, 1, 0, 3)]
    all_to_all x1, blocking collectives: 12.9 us -> 11.1 us  [spread(): return lax.all_to_all(x, axis, 0, 0, axis_index_groups=groups)]
    pallas_call x3 -> x5, Pallas kernels: 12.8 us -> 11.3 us  [the longest x1 8.03 us: local(): pl.pallas_call(split_kernel, grid=(parts,), out_shape=pltpu.HBM((parts, w...]
    another operation x1 -> x0, local copies, waits for them, and re-layouts: 1.33 us -> none  [local(): flat_exits[None, :]]
    pallas_call x1, Pallas kernels: 8.35 us -> 7.18 us  [local(): pl.pallas_call(lambda *refs: finish_kernel(local_reqs, scale, *refs), out...]
    reduce_sum x1 -> x0, other arithmetic: 0.97 us -> none  [local(): rank = jnp.sum((same & earlier).astype(jnp.int32), axis=-1)]
    unnamed x9 -> x15, local copies, waits for them, and re-layouts: 2.46 us -> 3.43 us
  transfers between devices with their start and end apart: 2 -> 2, of which waited for: 1 -> 2; matrix products, arithmetic and copies ran while one was open for 14% -> 3% of each run, Pallas kernels for 13% -> 16%
where the time goes in v3:
time: 62.3 us; the launch traced here: 61.8 us
  starting transfers between devices  24.6 us (39%)
  Pallas kernels  18.4 us (30%)
  blocking collectives  11.1 us (18%)
  local copies, waits for them, and re-layouts  3.69 us (6%)
  waiting for transfers between devices  2.2 us (4%)
  other arithmetic  0.97 us (2%)
  between operations  0.77 us (1%)
    all_to_all x1, starting transfers between devices, spread(): return lax.all_to_all(x, axis, 0, 0, axis_index_groups=groups)  15.7 us
    all_to_all x1, blocking collectives, spread(): return lax.all_to_all(x, axis, 0, 0, axis_index_groups=groups)  11.1 us
    ppermute x1, starting transfers between devices, local(): other = lax.ppermute(mine, 'tp', [(i, i ^ 1) for i in range(parts)])  8.89 us
    pallas_call x1, Pallas kernels, local(): pl.pallas_call(split_kernel, grid=(parts,), out_shape=pltpu.HBM((parts, w...  8.03 us
    pallas_call x1, Pallas kernels, local(): pl.pallas_call(lambda *refs: finish_kernel(local_reqs, scale, *refs), out...  7.18 us
    unnamed x15, local copies, waits for them, and re-layouts  3.43 us
    ppermute x1, waiting for transfers between devices, local(): other = lax.ppermute(mine, 'tp', [(i, i ^ 1) for i in range(parts)])  1.6 us
    pallas_call x1, Pallas kernels, local(): pl.pallas_call(lambda *refs: past_kernel(scale, *refs), out_shape=pltpu.V...  1.59 us
  transfers between devices with their start and end apart: 2, of which 2 were waited for; matrix products, arithmetic and copies ran while one was open for 3% of the time, Pallas kernels for 16%

profile of v3, /device:TPU:1, one launch (start us, length us, event | category | flops | bytes accessed | tf_op | source)
XLA Modules:
  0.0 61.8 jit_solution(17338265141614832020)
XLA Ops:
  0.6 0.0 copy-start.2
  0.6 0.9 %copy-done.2 = bf16[4,1,16,1024]{3,2,1,0:T(8,128)(2,1)S(1)} copy-done((bf16[4,1,16,1024]{3,2,1,0:T(8,128)(2,1)S(1)}, bf16[4,1,16,1024]{3,2,1,0:T(8,128)(2,1)}, u32[]{:S(2)}) %copy-start.2) | copy-done | bytes 131096
  1.5 0.7 %copy-done.4 = s32[4,16]{1,0:T(4,128)S(1)} copy-done((s32[4,16]{1,0:T(4,128)S(1)}, s32[4,16]{1,0:T(4,128)}, u32[]{:S(2)}) %copy-start.4) | copy-done | bytes 280
  2.2 1.1 %leaving.1 = bf16[16,8,1024]{2,1,0:T(8,128)(2,1)} custom-call(s32[1]{0:T(128)} %bitcast.7.section, s32[4,16]{1,0:T(4,128)S(1)} %copy-done.4, bf16[64,1024]{1,0:T(8,128)(2,1)S(1)} %bitcast.30), custom_call_target="tpu_custom_call" | custom-call | tf_op jit(solution)/shard_map/leaving/pallas_call | solution.py:207
  3.3 15.7 %all-to-all-start = ((bf16[16,8,1024]{2,1,0:T(8,128)(2,1)}), bf16[16,8,1024]{2,1,0:T(8,128)(2,1)S(1)}, u32[]{:S(2)}, u32[]{:S(2)}) async-start(bf16[16,8,1024]{2,1,0:T(8,128)(2,1)} %leaving.1), calls=%async_computation | async-start | bytes 524288 | tf_op jit(solution)/shard_map/all_to_all | solution.py:188
  19.0 0.0 copy-start.3
  19.1 0.9 %copy-done.3 = bf16[4,1,16,1024]{3,2,1,0:T(8,128)(2,1)S(1)} copy-done((bf16[4,1,16,1024]{3,2,1,0:T(8,128)(2,1)S(1)}, bf16[4,1,16,1024]{3,2,1,0:T(8,128)(2,1)}, u32[]{:S(2)}) %copy-start.3) | copy-done | bytes 131096
  19.9 0.4 choose.1
  20.3 0.7 %add_convert_fusion = f32[4,16]{1,0:T(4,128)S(1)} fusion(s32[16]{0:T(128)} %refs_0_.1), kind=kLoop, calls=%fused_computation.6 | loop fusion | flops 128 | bytes 320 | tf_op jit(solution)/shard_map/convert_element_type | solution.py:231
  21.0 0.1 convert_element_type.17
  21.1 0.1 reshape.71
  21.2 0.9 %copy.12 = bf16[8,8,8,128]{3,2,1,0:T(8,128)(2,1)S(1)} copy(bf16[8,8,8,128]{3,1,2,0:T(8,128)(2,1)} %bitcast.27) | data formatting | bytes 262144
  22.1 0.0 copy-start
  22.2 8.0 %split.1.refs_3_ = bf16[8,1024,256]{2,1,0:T(8,128)(2,1)} custom-call(bf16[16384,128]{1,0:T(8,128)(2,1)} %bitcast.32), custom_call_target="tpu_custom_call" | custom-call | tf_op jit(solution)/shard_map/split/pallas_call | solution.py:242
  30.2 1.6 %past.1.refs_5_ = f32[8,64,384]{2,1,0:T(8,128)S(1)} custom-call(s32[16]{0:T(128)S(1)} %copy-done.6, bf16[512,128]{1,0:T(8,128)(2,1)S(1)} %bitcast.29, bf16[16,2,128,128]{3,2,1,0:T(8,128)(2,1)S(1)} %bitcast.25), custom_call_target="tpu_custom_call" | custom-call | tf_op jit(solution)/shard_map/past/pallas_call | solution.py:251
  31.8 0.2 multiply_cosine_fusion
  32.0 0.1 maximum_bitcast_fusion
  32.1 0.1 stack_broadcast_in_dim.2
  32.2 0.6 all-to-all-done
  32.8 0.2 place.1
  33.0 11.1 %all_to_all.10.refs_1_ = bf16[4,72,1024]{2,1,0:T(8,128)(2,1)S(1)} all-to-all(bf16[4,72,1024]{2,1,0:T(8,128)(2,1)S(1)} %place.1), channel_id=1, replica_groups={{0,2,4,6},{1,3,5,7},{8,10,12,14},{9,11,13,15},{16,18,20,22},{17,19,21,2..., dimensions={0} | all-to-all | bytes 1179648 | tf_op jit(solution)/shard_map/all_to_all | solution.py:188
  44.1 8.9 %collective-permute-start = (bf16[4,72,1024]{2,1,0:T(8,128)(2,1)S(1)}, bf16[4,72,1024]{2,1,0:T(8,128)(2,1)S(1)}, u32[]{:S(2)}, u32[]{:S(2)}) collective-permute-start(bf16[4,72,1024]{2,1,0:T(8,128)(2,1)S(1)} %all_to_all.10.refs_1_), channel_id=1, source_target_pairs={{0,1},{1,0},{2,3},{3,2},{4,5},{5,4},{6,7},{7,6},{8,9},{9,8},{10,11... | collective-permute-start | bytes 1769480 | tf_op jit(solution)/shard_map/ppermute | solution.py:273
  53.0 1.6 %collective-permute-done.refs_2_ = bf16[4,72,1024]{2,1,0:T(8,128)(2,1)S(1)} collective-permute-done((bf16[4,72,1024]{2,1,0:T(8,128)(2,1)S(1)}, bf16[4,72,1024]{2,1,0:T(8,128)(2,1)S(1)}, u32[]{:S(2)}, u32[]{:S(2)}) %collective-permute-start) | collective-permute-done | bytes 589856 | tf_op jit(solution)/shard_map/ppermute | solution.py:273
  54.6 7.2 %finish.1 = (bf16[64,1024]{1,0:T(8,128)(2,1)}, bf16[128,128]{1,0:T(8,128)(2,1)}) custom-call(s32[1]{0:T(128)} %bitcast.refs_0_, bf16[4,72,1024]{2,1,0:T(8,128)(2,1)S(1)} %all_to_all.10.refs_1_, bf16[4,72,1024]{2,1,0:T(8,128)(2,1)S(1)} %collective-permute-done.refs_2_, bf16[8,1024,256]{2,1,0:T(8,128)(2,1)} %split.1.refs_3_, bf16[64,1024]{1,0:T(8,128)(2,1)S(1)} %bitcast.28, ...), custom_call_target="tpu_custom_call" | custom-call | tf_op jit(solution)/shard_map/finish/pallas_call | solution.py:275
  (12 shorter events, 0.1 us)
Async XLA Ops:
  0.6 0.9 %copy-start.2 = (bf16[4,1,16,1024]{3,2,1,0:T(8,128)(2,1)S(1)}, bf16[4,1,16,1024]{3,2,1,0:T(8,128)(2,1)}, u32[]{:S(2)}) copy-start(bf16[4,1,16,1024]{3,2,1,0:T(8,128)(2,1)} %param.7) | copy-start | bytes 393220
  1.5 0.7 %copy-start.4 = (s32[4,16]{1,0:T(4,128)S(1)}, s32[4,16]{1,0:T(4,128)}, u32[]{:S(2)}) copy-start(s32[4,16]{1,0:T(4,128)} %exits.3) | copy-start | bytes 772
  3.3 29.5 %all-to-all-start = ((bf16[16,8,1024]{2,1,0:T(8,128)(2,1)}), bf16[16,8,1024]{2,1,0:T(8,128)(2,1)S(1)}, u32[]{:S(2)}, u32[]{:S(2)}) async-start(bf16[16,8,1024]{2,1,0:T(8,128)(2,1)} %leaving.1), calls=%async_computation | async-start | bytes 524288 | tf_op jit(solution)/shard_map/all_to_all | solution.py:188
  19.0 0.9 %copy-start.3 = (bf16[4,1,16,1024]{3,2,1,0:T(8,128)(2,1)S(1)}, bf16[4,1,16,1024]{3,2,1,0:T(8,128)(2,1)}, u32[]{:S(2)}) copy-start(bf16[4,1,16,1024]{3,2,1,0:T(8,128)(2,1)} %param.7) | copy-start | bytes 393220
  22.1 8.1 %copy-start = (bf16[1,16,2,128,128]{4,3,2,1,0:T(8,128)(2,1)S(1)}, bf16[1,16,2,128,128]{4,3,2,1,0:T(8,128)(2,1)}, u32[]{:S(2)}) copy-start(bf16[1,16,2,128,128]{4,3,2,1,0:T(8,128)(2,1)} %param.11) | copy-start | bytes 3145732
  22.2 8.1 %copy-start.6 = (s32[16]{0:T(128)S(1)}, s32[16]{0:T(128)}, u32[]{:S(2)}) copy-start(s32[16]{0:T(128)} %refs_0_.1) | copy-start | bytes 196
  22.2 10.7 %copy-start.5 = (bf16[1,1024]{1,0:T(2,128)(2,1)S(1)}, bf16[1,1024]{1,0:T(2,128)(2,1)}, u32[]{:S(2)}) copy-start(bf16[1,1024]{1,0:T(2,128)(2,1)} %gain.1) | copy-start | bytes 6148
  30.2 24.4 %copy-start.1 = (bf16[4,1,16,1024]{3,2,1,0:T(8,128)(2,1)S(1)}, bf16[4,1,16,1024]{3,2,1,0:T(8,128)(2,1)}, u32[]{:S(2)}) copy-start(bf16[4,1,16,1024]{3,2,1,0:T(8,128)(2,1)} %param.10) | copy-start | bytes 393220
  44.1 10.5 %collective-permute-start = (bf16[4,72,1024]{2,1,0:T(8,128)(2,1)S(1)}, bf16[4,72,1024]{2,1,0:T(8,128)(2,1)S(1)}, u32[]{:S(2)}, u32[]{:S(2)}) collective-permute-start(bf16[4,72,1024]{2,1,0:T(8,128)(2,1)S(1)} %all_to_all.10.refs_1_), channel_id=1, source_target_pairs={{0,1},{1,0},{2,3},{3,2},{4,5},{5,4},{6,7},{7,6},{8,9},{9,8},{10,11... | collective-permute-start | bytes 1769480 | tf_op jit(solution)/shard_map/ppermute | solution.py:273

commit v4 on v3

--- a/solution.py
+++ b/solution.py
@@ -8,13 +8,14 @@
 D = 8192
 HEAD = 128
 EXIT_CAP = 2
-GAIN_ROWS = 8
+EXTRA = 16
 
 
 EPSILON = 1e-05
 ROPE_BASE = 500000.0
 VMEM = pl.BlockSpec(memory_space=pltpu.VMEM)
 SMEM = pl.BlockSpec(memory_space=pltpu.SMEM)
+HBM = pl.BlockSpec(memory_space=pltpu.HBM)
 
 
 def iota(shape, axis):
@@ -39,9 +40,15 @@
     return exact(as_bf16(same), as_bf16(before))
 
 
-def leaving_kernel(section, exits, own, out):
+def leaving_kernel(section, exits_far, own_far, out, exits, own, chosen, sems):
     steps, reqs = exits.shape
     rows = own.shape[0]
+    copies = out.shape[0]
+    load_exits = pltpu.make_async_copy(exits_far, exits, sems.at[copies])
+    load_own = pltpu.make_async_copy(own_far, own, sems.at[copies + 1])
+    load_exits.start()
+    load_own.start()
+    load_exits.wait()
     here = exits[...] == section[0]
     rank = ranks(here)
     picks = [here & (rank == k) for k in range(EXIT_CAP)]
@@ -51,9 +58,13 @@
     slots = EXIT_CAP * steps
     match = iota((slots, rows), 0) % steps == iota((slots, rows), 1) // reqs
     wide = jnp.where(match, wide, 0.0).astype(jnp.bfloat16)
-    chosen = exact(wide, own[...]).astype(jnp.bfloat16)
-    for k in range(out.shape[0]):
-        out[k] = chosen
+    load_own.wait()
+    chosen[...] = exact(wide, own[...]).astype(jnp.bfloat16)
+    stores = [pltpu.make_async_copy(chosen, out.at[k], sems.at[k]) for k in range(copies)]
+    for store in stores:
+        store.start()
+    for store in stores:
+        store.wait()
 
 
 def choose_kernel(section, exits, own, take, kept):
@@ -110,14 +121,37 @@
                 out[g, row, 2 * HEAD : 3 * HEAD] = total[at]
 
 
+def diagonal(rows):
+    return iota((rows, HEAD), 0) == iota((rows, HEAD), 1)
+
+
 def place_kernel(take, kept, arrived, gain, out):
-    rows = kept.shape[0]
-    source = jnp.dot(take[...], arrived[...], preferred_element_type=jnp.float32)
+    rows, width = kept.shape
+    blocks = width // HEAD
+    source = exact(take[...], arrived[...])
     source = (source + kept[...].astype(jnp.float32)).astype(jnp.bfloat16)
-    gains = jnp.broadcast_to(gain[...], (GAIN_ROWS, gain.shape[1]))
+    values = source.astype(jnp.float32)
+    squares = jnp.zeros((rows, HEAD), jnp.float32)
+    for j in range(blocks):
+        value = values[:, HEAD * j : HEAD * (j + 1)]
+        squares = squares + value * value
+    squares = jnp.sum(squares, axis=-1, keepdims=True)
+    squares = jnp.sum(jnp.where(diagonal(rows), squares, 0.0), axis=0, keepdims=True)
+    high = squares.astype(jnp.bfloat16).astype(jnp.float32)
+    middle = (squares - high).astype(jnp.bfloat16).astype(jnp.float32)
+    low = squares - high - middle
+    at = iota((8, HEAD), 0)
+    sums = jnp.zeros((8, HEAD), jnp.float32)
+    for k, piece in enumerate((high, middle, low)):
+        sums = jnp.where(at == k, piece, sums)
+    gains = jnp.zeros((8, HEAD), jnp.float32)
+    for j in range(blocks):
+        gains = jnp.where(at == j, gain[:, HEAD * j : HEAD * (j + 1)].astype(jnp.float32), gains)
+    extra = jnp.concatenate([gains, sums], axis=0).astype(jnp.bfloat16)
     for k in range(out.shape[0]):
-        out[k, 0:rows, :] = source
-        out[k, rows : rows + GAIN_ROWS, :] = gains
+        for j in range(blocks):
+            out[k, rows * j : rows * (j + 1), :] = source[:, HEAD * j : HEAD * (j + 1)]
+        out[k, rows * blocks : rows * blocks + EXTRA, :] = extra
 
 
 def finish_kernel(
@@ -125,7 +159,7 @@
 ):
     rows = queries.shape[0]
     chips = mine.shape[0]
-    width = mine.shape[2]
+    blocks = weight.shape[1] // HEAD
     order = [(mine, x, 2 * x + core[0]) for x in range(chips)]
     order += [(other, x, 2 * x + 1 - core[0]) for x in range(chips)]
     loads = [
@@ -134,46 +168,54 @@
     ]
     for load in loads:
         load.start()
-    squares = jnp.zeros((rows, HEAD), jnp.float32)
-    for held in (mine, other):
-        for x in range(chips):
-            for j in range(width // HEAD):
-                value = held[x, 0:rows, HEAD * j : HEAD * (j + 1)].astype(jnp.float32)
-                squares = squares + value * value
-    mean = jnp.sum(squares, axis=-1, keepdims=True) / D
-    inverse = lax.rsqrt(mean + EPSILON)
+    squares = jnp.zeros((8, HEAD), jnp.float32)
+    extras = []
+    for held, x, _ in order:
+        extra = held[x, rows * blocks : rows * blocks + EXTRA, :].astype(jnp.float32)
+        extras.append(extra[:8])
+        squares = squares + extra[8:]
+    squares = jnp.sum(squares, axis=0, keepdims=True)
+    squares = jnp.sum(jnp.where(diagonal(rows), squares, 0.0), axis=-1, keepdims=True)
+    inverse = lax.rsqrt(squares / D + EPSILON)
     pairs = jnp.zeros((rows, 2 * HEAD), jnp.float32)
     for i, (held, x, _) in enumerate(order):
-        value = held[x, 0:rows, :].astype(jnp.float32)
-        gain = held[x, rows : rows + 1, :].astype(jnp.float32)
-        normed = (value * inverse * gain).astype(jnp.bfloat16)
+        normed = []
+        for j in range(blocks):
+            value = held[x, rows * j : rows * (j + 1), :].astype(jnp.float32)
+            normed.append((value * inverse * extras[i][j : j + 1]).astype(jnp.bfloat16))
         loads[i].wait()
-        pairs = pairs + exact(normed, held_weight[i])
+        pairs = pairs + exact(jnp.concatenate(normed, axis=1), held_weight[i])
     keys = pairs[:, :HEAD]
     turned = pltpu.roll(keys, HEAD // 2, 1)
     new_keys = (keys * table[0] + turned * table[1]).astype(jnp.bfloat16)
     new_values = pairs[:, HEAD:].astype(jnp.bfloat16)
-    to, fro = iota((2 * rows, 2 * rows), 0), iota((2 * rows, 2 * rows), 1)
-    weave = (fro == (to // 2) + rows * (to % 2)).astype(jnp.float32).astype(jnp.bfloat16)
-    stacked = jnp.concatenate([new_keys, new_values], axis=0)
-    out_kv[...] = jnp.dot(weave, stacked, preferred_element_type=jnp.float32).astype(jnp.bfloat16)
-    by, of = iota((rows, rows), 0), iota((rows, rows), 1)
+    padding = jnp.zeros((HEAD - rows, HEAD), jnp.bfloat16)
+    wide_keys = jnp.concatenate([new_keys, padding], axis=0)
+    wide_values = jnp.concatenate([new_values, padding], axis=0)
+    by, of = iota((rows, HEAD), 0), iota((rows, HEAD), 1)
     seen = (by % reqs == of % reqs) & (of // reqs <= by // reqs)
     live = table[2]
     for g in range(old.shape[0]):
         span = slice(g * HEAD, (g + 1) * HEAD)
-        scores = contract_last(queries[:, span], new_keys) * scale
+        scores = contract_last(queries[:, span], wide_keys) * scale
         scores = jnp.where(seen, scores, -1e30)
-        before, old_top, old_total = old[g, :, 0:HEAD], old[g, :, HEAD : HEAD + 1], old[g, :, 2 * HEAD : 2 * HEAD + 1]
+        old_top = old[g, :, HEAD : 2 * HEAD]
         top = jnp.maximum(old_top, jnp.max(scores, axis=-1, keepdims=True))
         shrink = jnp.exp(old_top - top)
         grown = jnp.exp(scores - top)
-        total = shrink * old_total + jnp.sum(grown, axis=-1, keepdims=True)
-        fresh = (grown / total).astype(jnp.bfloat16)
-        mixed = before * (shrink / total) + jnp.dot(
-            fresh, new_values, preferred_element_type=jnp.float32
-        )
+        total = shrink * old[g, :, 2 * HEAD :] + jnp.sum(grown, axis=-1, keepdims=True)
+        part = 1.0 / total
+        fresh = (grown * part).astype(jnp.bfloat16)
+        mixed = old[g, :, 0:HEAD] * (shrink * part) + exact(fresh, wide_values)
         out_attn[:, span] = (mixed * live).astype(jnp.bfloat16)
+    to, fro = iota((2 * rows, 2 * rows), 0), iota((2 * rows, 2 * rows), 1)
+    weave = as_bf16(fro == (to // 2) + rows * (to % 2))
+    stacked = jnp.concatenate([new_keys, new_values], axis=0)
+    out_kv[...] = exact(weave, stacked).astype(jnp.bfloat16)
+
+
+def far(x):
+    return pltpu.with_memory_space_constraint(x, pltpu.HBM)
 
 
 def near(x):
@@ -206,12 +248,18 @@
     section_scalar = section_index.reshape(1)
     outgoing = pl.pallas_call(
         leaving_kernel,
-        out_shape=pltpu.VMEM((sections, slots, width), jnp.bfloat16),
-        in_specs=[SMEM, VMEM, VMEM],
-        out_specs=VMEM,
+        out_shape=pltpu.HBM((sections, slots, width), jnp.bfloat16),
+        in_specs=[SMEM, HBM, HBM],
+        out_specs=HBM,
+        scratch_shapes=[
+            pltpu.VMEM(exits.shape, jnp.int32),
+            pltpu.VMEM(own.shape, jnp.bfloat16),
+            pltpu.VMEM((slots, width), jnp.bfloat16),
+            pltpu.SemaphoreType.DMA((sections + 2,)),
+        ],
         compiler_params=small(4),
         name="leaving",
-    )(section_scalar, exits, own)
+    )(section_scalar, far(exits), far(own))
     arrived = spread(outgoing, "section").reshape(sections * slots, width)
 
     take, kept = pl.pallas_call(
@@ -247,7 +295,7 @@
         out_specs=pl.BlockSpec((1, width, 2 * HEAD), lambda i: (i, 0, 0)),
         compiler_params=small(8),
         name="split",
-    )(pltpu.with_memory_space_constraint(w_kv.reshape(2 * D, HEAD), pltpu.HBM))
+    )(far(w_kv.reshape(2 * D, HEAD)))
     old = pl.pallas_call(
         lambda *refs: past_kernel(scale, *refs),
         out_shape=pltpu.VMEM((groups, rows, 3 * HEAD), jnp.float32),
@@ -262,7 +310,7 @@
     )
     sent = pl.pallas_call(
         place_kernel,
-        out_shape=pltpu.VMEM((chips, rows + GAIN_ROWS, width), jnp.bfloat16),
+        out_shape=pltpu.VMEM((chips, rows * (width // HEAD) + EXTRA, HEAD), jnp.bfloat16),
         in_specs=[VMEM] * 4,
         out_specs=VMEM,
         compiler_params=small(4),
@@ -278,7 +326,7 @@
             jax.ShapeDtypeStruct((rows, groups * HEAD), jnp.bfloat16),
             jax.ShapeDtypeStruct((2 * rows, HEAD), jnp.bfloat16),
         ),
-        in_specs=[SMEM, VMEM, VMEM, pl.BlockSpec(memory_space=pltpu.HBM)] + [VMEM] * 3,
+        in_specs=[SMEM, VMEM, VMEM, HBM] + [VMEM] * 3,
         out_specs=(VMEM, VMEM),
         scratch_shapes=[
             pltpu.VMEM((parts, width, 2 * HEAD), jnp.bfloat16),
@@ -290,7 +338,7 @@
         core.reshape(1),
         near(mine),
         near(other),
-        pltpu.with_memory_space_constraint(weight, pltpu.HBM),
+        far(weight),
         near(queries.reshape(rows, groups * HEAD)),
         near(old),
         near(table),

time: 62.3 us -> 60.1 us (0.965)
  local copies, waits for them, and re-layouts: 3.69 us -> 2.8 us
  waiting for transfers between devices: 2.2 us -> 1.53 us
    pallas_call x1, Pallas kernels: 7.18 us -> 5.97 us  [local(): pl.pallas_call(lambda *refs: finish_kernel(local_reqs, scale, *refs), out...]
    pallas_call x2, Pallas kernels: 1.25 us -> 2.19 us  [the longest x1 1.92 us: local(): pl.pallas_call(leaving_kernel, out_shape=pltpu.HBM((sections, slots, widt...]
    unnamed x15 -> x13, local copies, waits for them, and re-layouts: 3.43 us -> 2.53 us
  transfers between devices with their start and end apart: 2 -> 2, of which waited for: 2 -> 1; matrix products, arithmetic and copies ran while one was open for 3% -> 4% of each run, Pallas kernels for 16% -> 17%
where the time goes in v4:
time: 60.1 us; the launch traced here: 59.6 us
  starting transfers between devices  24.5 us (41%)
  Pallas kernels  18.2 us (30%)
  blocking collectives  10.8 us (18%)
  local copies, waits for them, and re-layouts  2.8 us (5%)
  waiting for transfers between devices  1.53 us (3%)
  other arithmetic  0.97 us (2%)
  between operations  0.78 us (1%)
    all_to_all x1, starting transfers between devices, spread(): return lax.all_to_all(x, axis, 0, 0, axis_index_groups=groups)  15.7 us
    all_to_all x1, blocking collectives, spread(): return lax.all_to_all(x, axis, 0, 0, axis_index_groups=groups)  10.8 us
    ppermute x1, starting transfers between devices, local(): other = lax.ppermute(mine, 'tp', [(i, i ^ 1) for i in range(parts)])  8.77 us
    pallas_call x1, Pallas kernels, local(): pl.pallas_call(split_kernel, grid=(parts,), out_shape=pltpu.HBM((parts, w...  8.05 us
    pallas_call x1, Pallas kernels, local(): pl.pallas_call(lambda *refs: finish_kernel(local_reqs, scale, *refs), out...  5.97 us
    unnamed x13, local copies, waits for them, and re-layouts  2.53 us
    pallas_call x1, Pallas kernels, local(): pl.pallas_call(leaving_kernel, out_shape=pltpu.HBM((sections, slots, widt...  1.92 us
    pallas_call x1, Pallas kernels, local(): pl.pallas_call(lambda *refs: past_kernel(scale, *refs), out_shape=pltpu.V...  1.59 us
  transfers between devices with their start and end apart: 2, of which 1 were waited for; matrix products, arithmetic and copies ran while one was open for 4% of the time, Pallas kernels for 17%

profile of v4, /device:TPU:1, one launch (start us, length us, event | category | flops | bytes accessed | tf_op | source)
XLA Modules:
  0.0 59.6 jit_solution(1598562904106314147)
XLA Ops:
  0.6 1.9 %leaving.1 = bf16[16,8,1024]{2,1,0:T(8,128)(2,1)} custom-call(s32[1]{0:T(128)} %bitcast.7.section, s32[4,16]{1,0:T(4,128)} %exits_far.1, bf16[64,1024]{1,0:T(8,128)(2,1)} %bitcast.30), custom_call_target="tpu_custom_call" | custom-call | tf_op jit(solution)/shard_map/leaving/pallas_call | solution.py:249
  2.6 15.7 %all-to-all-start = ((bf16[16,8,1024]{2,1,0:T(8,128)(2,1)}), bf16[16,8,1024]{2,1,0:T(8,128)(2,1)S(1)}, u32[]{:S(2)}, u32[]{:S(2)}) async-start(bf16[16,8,1024]{2,1,0:T(8,128)(2,1)} %leaving.1), calls=%async_computation | async-start | bytes 524288 | tf_op jit(solution)/shard_map/all_to_all | solution.py:230
  18.3 0.0 copy-start.2
  18.3 0.9 %copy-done.2 = bf16[4,1,16,1024]{3,2,1,0:T(8,128)(2,1)S(1)} copy-done((bf16[4,1,16,1024]{3,2,1,0:T(8,128)(2,1)S(1)}, bf16[4,1,16,1024]{3,2,1,0:T(8,128)(2,1)}, u32[]{:S(2)}) %copy-start.2) | copy-done | bytes 131096
  19.2 0.7 %copy-done.3 = s32[4,16]{1,0:T(4,128)S(1)} copy-done((s32[4,16]{1,0:T(4,128)S(1)}, s32[4,16]{1,0:T(4,128)}, u32[]{:S(2)}) %copy-start.3) | copy-done | bytes 280
  19.9 0.4 choose.1
  20.3 0.7 %add_convert_fusion = f32[4,16]{1,0:T(4,128)S(1)} fusion(s32[16]{0:T(128)} %refs_0_.1), kind=kLoop, calls=%fused_computation.6 | loop fusion | flops 128 | bytes 320 | tf_op jit(solution)/shard_map/convert_element_type | solution.py:279
  21.0 0.1 convert_element_type.17
  21.0 0.1 reshape.71
  21.1 0.9 %copy.12 = bf16[8,8,8,128]{3,2,1,0:T(8,128)(2,1)S(1)} copy(bf16[8,8,8,128]{3,1,2,0:T(8,128)(2,1)} %bitcast.27) | data formatting | bytes 262144
  22.1 0.0 copy-start
  22.1 0.0 copy-start.5
  22.1 0.0 copy-start.4
  22.1 8.0 %split.1.refs_3_ = bf16[8,1024,256]{2,1,0:T(8,128)(2,1)} custom-call(bf16[16384,128]{1,0:T(8,128)(2,1)} %bitcast.32), custom_call_target="tpu_custom_call" | custom-call | tf_op jit(solution)/shard_map/split/pallas_call | solution.py:290
  30.2 1.6 %past.1.refs_5_ = f32[8,64,384]{2,1,0:T(8,128)S(1)} custom-call(s32[16]{0:T(128)S(1)} %copy-done.5, bf16[512,128]{1,0:T(8,128)(2,1)S(1)} %bitcast.29, bf16[16,2,128,128]{3,2,1,0:T(8,128)(2,1)S(1)} %bitcast.25), custom_call_target="tpu_custom_call" | custom-call | tf_op jit(solution)/shard_map/past/pallas_call | solution.py:299
  31.8 0.2 multiply_cosine_fusion
  32.0 0.1 maximum_bitcast_fusion
  32.1 0.1 stack_broadcast_in_dim.2
  32.2 0.0 all-to-all-done
  32.2 0.3 place.1
  32.5 10.8 %all_to_all.10.refs_1_ = bf16[4,528,128]{2,1,0:T(8,128)(2,1)S(1)} all-to-all(bf16[4,528,128]{2,1,0:T(8,128)(2,1)S(1)} %place.1), channel_id=1, replica_groups={{0,2,4,6},{1,3,5,7},{8,10,12,14},{9,11,13,15},{16,18,20,22},{17,19,21,2..., dimensions={0} | all-to-all | bytes 1081344 | tf_op jit(solution)/shard_map/all_to_all | solution.py:230
  43.3 8.8 %collective-permute-start = (bf16[4,528,128]{2,1,0:T(8,128)(2,1)S(1)}, bf16[4,528,128]{2,1,0:T(8,128)(2,1)S(1)}, u32[]{:S(2)}, u32[]{:S(2)}) collective-permute-start(bf16[4,528,128]{2,1,0:T(8,128)(2,1)S(1)} %all_to_all.10.refs_1_), channel_id=1, source_target_pairs={{0,1},{1,0},{2,3},{3,2},{4,5},{5,4},{6,7},{7,6},{8,9},{9,8},{10,11... | collective-permute-start | bytes 1622024 | tf_op jit(solution)/shard_map/ppermute | solution.py:321
  52.1 1.5 %collective-permute-done.refs_2_ = bf16[4,528,128]{2,1,0:T(8,128)(2,1)S(1)} collective-permute-done((bf16[4,528,128]{2,1,0:T(8,128)(2,1)S(1)}, bf16[4,528,128]{2,1,0:T(8,128)(2,1)S(1)}, u32[]{:S(2)}, u32[]{:S(2)}) %collective-permute-start) | collective-permute-done | bytes 540704 | tf_op jit(solution)/shard_map/ppermute | solution.py:321
  53.6 6.0 %finish.1 = (bf16[64,1024]{1,0:T(8,128)(2,1)}, bf16[128,128]{1,0:T(8,128)(2,1)}) custom-call(s32[1]{0:T(128)} %bitcast.refs_0_, bf16[4,528,128]{2,1,0:T(8,128)(2,1)S(1)} %all_to_all.10.refs_1_, bf16[4,528,128]{2,1,0:T(8,128)(2,1)S(1)} %collective-permute-done.refs_2_, bf16[8,1024,256]{2,1,0:T(8,128)(2,1)} %split.1.refs_3_, bf16[64,1024]{1,0:T(8,128)(2,1)S(1)} %bitcast.28, ...), custom_call_target="tpu_custom_call" | custom-call | tf_op jit(solution)/shard_map/finish/pallas_call | solution.py:323
  (10 shorter events, 0.1 us)
Async XLA Ops:
  2.6 29.6 %all-to-all-start = ((bf16[16,8,1024]{2,1,0:T(8,128)(2,1)}), bf16[16,8,1024]{2,1,0:T(8,128)(2,1)S(1)}, u32[]{:S(2)}, u32[]{:S(2)}) async-start(bf16[16,8,1024]{2,1,0:T(8,128)(2,1)} %leaving.1), calls=%async_computation | async-start | bytes 524288 | tf_op jit(solution)/shard_map/all_to_all | solution.py:230
  18.3 0.9 %copy-start.2 = (bf16[4,1,16,1024]{3,2,1,0:T(8,128)(2,1)S(1)}, bf16[4,1,16,1024]{3,2,1,0:T(8,128)(2,1)}, u32[]{:S(2)}) copy-start(bf16[4,1,16,1024]{3,2,1,0:T(8,128)(2,1)} %param.7) | copy-start | bytes 393220
  19.2 0.7 %copy-start.3 = (s32[4,16]{1,0:T(4,128)S(1)}, s32[4,16]{1,0:T(4,128)}, u32[]{:S(2)}) copy-start(s32[4,16]{1,0:T(4,128)} %exits_far.1) | copy-start | bytes 772
  22.1 8.1 %copy-start = (bf16[1,16,2,128,128]{4,3,2,1,0:T(8,128)(2,1)S(1)}, bf16[1,16,2,128,128]{4,3,2,1,0:T(8,128)(2,1)}, u32[]{:S(2)}) copy-start(bf16[1,16,2,128,128]{4,3,2,1,0:T(8,128)(2,1)} %param.11) | copy-start | bytes 3145732
  22.1 8.1 %copy-start.5 = (s32[16]{0:T(128)S(1)}, s32[16]{0:T(128)}, u32[]{:S(2)}) copy-start(s32[16]{0:T(128)} %refs_0_.1) | copy-start | bytes 196
  22.1 10.1 %copy-start.4 = (bf16[1,1024]{1,0:T(2,128)(2,1)S(1)}, bf16[1,1024]{1,0:T(2,128)(2,1)}, u32[]{:S(2)}) copy-start(bf16[1,1024]{1,0:T(2,128)(2,1)} %gain.1) | copy-start | bytes 6148
  30.2 23.5 %copy-start.1 = (bf16[4,1,16,1024]{3,2,1,0:T(8,128)(2,1)S(1)}, bf16[4,1,16,1024]{3,2,1,0:T(8,128)(2,1)}, u32[]{:S(2)}) copy-start(bf16[4,1,16,1024]{3,2,1,0:T(8,128)(2,1)} %param.10) | copy-start | bytes 393220
  43.3 10.3 %collective-permute-start = (bf16[4,528,128]{2,1,0:T(8,128)(2,1)S(1)}, bf16[4,528,128]{2,1,0:T(8,128)(2,1)S(1)}, u32[]{:S(2)}, u32[]{:S(2)}) collective-permute-start(bf16[4,528,128]{2,1,0:T(8,128)(2,1)S(1)} %all_to_all.10.refs_1_), channel_id=1, source_target_pairs={{0,1},{1,0},{2,3},{3,2},{4,5},{5,4},{6,7},{7,6},{8,9},{9,8},{10,11... | collective-permute-start | bytes 1622024 | tf_op jit(solution)/shard_map/ppermute | solution.py:321

commit v5 on v4

--- a/solution.py
+++ b/solution.py
@@ -8,7 +8,7 @@
 D = 8192
 HEAD = 128
 EXIT_CAP = 2
-EXTRA = 16
+EXTRA = 8
 
 
 EPSILON = 1e-05
@@ -87,14 +87,14 @@
     kept[...] = jnp.where(column >= 0.0, 0.0, own[...].astype(jnp.float32)).astype(jnp.bfloat16)
 
 
-def split_kernel(weight, out):
-    half = 128
-    to, fro = iota((2 * half, 2 * half), 0), iota((2 * half, 2 * half), 1)
-    split = as_bf16(fro == jnp.where(to < half, 2 * to, 2 * (to - half) + 1))
-    for j in range(weight.shape[0] // (2 * half)):
-        pair = exact(split, weight[2 * half * j : 2 * half * (j + 1), :]).astype(jnp.bfloat16)
-        out[0, half * j : half * (j + 1), 0:HEAD] = pair[:half]
-        out[0, half * j : half * (j + 1), HEAD : 2 * HEAD] = pair[half:]
+def split_kernel(weight, out, wide):
+    rows = weight.shape[0] // 2
+    wide[...] = weight[...].astype(jnp.float32)
+    for k in range(2):
+        half = wide[pl.ds(k, rows, stride=2), :].astype(jnp.bfloat16)
+        for p in range(out.shape[0]):
+            part = half[p * out.shape[1] : (p + 1) * out.shape[1]]
+            out[p, :, HEAD * k : HEAD * (k + 1)] = part
 
 
 def past_kernel(scale, lengths, queries, cache, out):
@@ -140,51 +140,57 @@
     high = squares.astype(jnp.bfloat16).astype(jnp.float32)
     middle = (squares - high).astype(jnp.bfloat16).astype(jnp.float32)
     low = squares - high - middle
-    at = iota((8, HEAD), 0)
-    sums = jnp.zeros((8, HEAD), jnp.float32)
+    at = iota((EXTRA, HEAD), 0)
+    sums = jnp.zeros((EXTRA, HEAD), jnp.float32)
     for k, piece in enumerate((high, middle, low)):
         sums = jnp.where(at == k, piece, sums)
-    gains = jnp.zeros((8, HEAD), jnp.float32)
-    for j in range(blocks):
-        gains = jnp.where(at == j, gain[:, HEAD * j : HEAD * (j + 1)].astype(jnp.float32), gains)
-    extra = jnp.concatenate([gains, sums], axis=0).astype(jnp.bfloat16)
+    scaled = (values * gain[...].astype(jnp.float32)).astype(jnp.bfloat16)
+    extra = sums.astype(jnp.bfloat16)
     for k in range(out.shape[0]):
         for j in range(blocks):
-            out[k, rows * j : rows * (j + 1), :] = source[:, HEAD * j : HEAD * (j + 1)]
+            out[k, rows * j : rows * (j + 1), :] = scaled[:, HEAD * j : HEAD * (j + 1)]
         out[k, rows * blocks : rows * blocks + EXTRA, :] = extra
 
 
-def finish_kernel(
-    reqs, scale, core, mine, other, weight, queries, old, table, out_attn, out_kv, held_weight, sems
-):
+def gathered(held, x, rows, blocks):
+    return jnp.concatenate([held[x, rows * j : rows * (j + 1), :] for j in range(blocks)], axis=1)
+
+
+def half_kernel(core, held, weight, pairs, ahead, mine, sems):
+    chips = held.shape[0]
+    blocks = weight.shape[1] // HEAD
+    rows = pairs.shape[0]
+    loads = [pltpu.make_async_copy(weight.at[2 * x + core[0]], mine.at[x], sems.at[x]) for x in range(chips)]
+    more = [
+        pltpu.make_async_copy(weight.at[2 * x + 1 - core[0]], ahead.at[x], sems.at[chips + x])
+        for x in range(chips)
+    ]
+    for load in loads + more:
+        load.start()
+    total = jnp.zeros(pairs.shape, jnp.float32)
+    for x in range(chips):
+        loads[x].wait()
+        total = total + exact(gathered(held, x, rows, blocks), mine[x])
+    pairs[...] = total
+    for load in more:
+        load.wait()
+
+
+def finish_kernel(reqs, scale, mine, other, pairs, weight, queries, old, table, out_attn, out_kv):
     rows = queries.shape[0]
     chips = mine.shape[0]
     blocks = weight.shape[1] // HEAD
-    order = [(mine, x, 2 * x + core[0]) for x in range(chips)]
-    order += [(other, x, 2 * x + 1 - core[0]) for x in range(chips)]
-    loads = [
-        pltpu.make_async_copy(weight.at[part], held_weight.at[i], sems.at[i])
-        for i, (_, _, part) in enumerate(order)
-    ]
-    for load in loads:
-        load.start()
-    squares = jnp.zeros((8, HEAD), jnp.float32)
-    extras = []
-    for held, x, _ in order:
-        extra = held[x, rows * blocks : rows * blocks + EXTRA, :].astype(jnp.float32)
-        extras.append(extra[:8])
-        squares = squares + extra[8:]
+    squares = jnp.zeros((EXTRA, HEAD), jnp.float32)
+    for held in (mine, other):
+        for x in range(chips):
+            squares = squares + held[x, rows * blocks : rows * blocks + EXTRA, :].astype(jnp.float32)
     squares = jnp.sum(squares, axis=0, keepdims=True)
     squares = jnp.sum(jnp.where(diagonal(rows), squares, 0.0), axis=-1, keepdims=True)
     inverse = lax.rsqrt(squares / D + EPSILON)
-    pairs = jnp.zeros((rows, 2 * HEAD), jnp.float32)
-    for i, (held, x, _) in enumerate(order):
-        normed = []
-        for j in range(blocks):
-            value = held[x, rows * j : rows * (j + 1), :].astype(jnp.float32)
-            normed.append((value * inverse * extras[i][j : j + 1]).astype(jnp.bfloat16))
-        loads[i].wait()
-        pairs = pairs + exact(jnp.concatenate(normed, axis=1), held_weight[i])
+    pairs = pairs[...]
+    for x in range(chips):
+        pairs = pairs + exact(gathered(other, x, rows, blocks), weight[x])
+    pairs = pairs * inverse
     keys = pairs[:, :HEAD]
     turned = pltpu.roll(keys, HEAD // 2, 1)
     new_keys = (keys * table[0] + turned * table[1]).astype(jnp.bfloat16)
@@ -289,11 +295,12 @@
     by_request = queries.reshape(num_steps, local_reqs, groups, HEAD).transpose(1, 0, 2, 3)
     weight = pl.pallas_call(
         split_kernel,
-        grid=(parts,),
+        grid=(chips,),
         out_shape=pltpu.HBM((parts, width, 2 * HEAD), jnp.bfloat16),
-        in_specs=[pl.BlockSpec((2 * width, HEAD), lambda i: (i, 0))],
-        out_specs=pl.BlockSpec((1, width, 2 * HEAD), lambda i: (i, 0, 0)),
-        compiler_params=small(8),
+        in_specs=[pl.BlockSpec((4 * width, HEAD), lambda i: (i, 0))],
+        out_specs=pl.BlockSpec((2, width, 2 * HEAD), lambda i: (i, 0, 0)),
+        scratch_shapes=[pltpu.VMEM((4 * width, HEAD), jnp.float32)],
+        compiler_params=small(16),
         name="split",
     )(far(w_kv.reshape(2 * D, HEAD)))
     old = pl.pallas_call(
@@ -320,25 +327,36 @@
     mine = spread(sent, "tp", same_core)
     other = lax.ppermute(mine, "tp", [(i, i ^ 1) for i in range(parts)])
 
+    pairs, ahead = pl.pallas_call(
+        half_kernel,
+        out_shape=(
+            pltpu.VMEM((rows, 2 * HEAD), jnp.float32),
+            pltpu.VMEM((chips, width, 2 * HEAD), jnp.bfloat16),
+        ),
+        in_specs=[SMEM, VMEM, HBM],
+        out_specs=(VMEM, VMEM),
+        scratch_shapes=[
+            pltpu.VMEM((chips, width, 2 * HEAD), jnp.bfloat16),
+            pltpu.SemaphoreType.DMA((parts,)),
+        ],
+        compiler_params=small(16),
+        name="half",
+    )(core.reshape(1), near(mine), far(weight))
     attended, fresh = pl.pallas_call(
         lambda *refs: finish_kernel(local_reqs, scale, *refs),
         out_shape=(
             jax.ShapeDtypeStruct((rows, groups * HEAD), jnp.bfloat16),
             jax.ShapeDtypeStruct((2 * rows, HEAD), jnp.bfloat16),
         ),
-        in_specs=[SMEM, VMEM, VMEM, HBM] + [VMEM] * 3,
+        in_specs=[VMEM] * 7,
         out_specs=(VMEM, VMEM),
-        scratch_shapes=[
-            pltpu.VMEM((parts, width, 2 * HEAD), jnp.bfloat16),
-            pltpu.SemaphoreType.DMA((parts,)),
-        ],
-        compiler_params=small(24),
+        compiler_params=small(16),
         name="finish",
     )(
-        core.reshape(1),
         near(mine),
         near(other),
-        far(weight),
+        near(pairs),
+        near(ahead),
         near(queries.reshape(rows, groups * HEAD)),
         near(old),
         near(table),

time: 60.1 us -> 58.6 us (0.975)
  Pallas kernels: 18.2 us -> 15.5 us
  other arithmetic: 0.97 us -> 1.65 us
    pallas_call x1, Pallas kernels: 5.97 us -> 3.85 us  [local(): pl.pallas_call(lambda *refs: finish_kernel(local_reqs, scale, *refs), out...]
    all_to_all x1, waiting for transfers between devices: 0.01 us -> 1.99 us  [spread(): return lax.all_to_all(x, axis, 0, 0, axis_index_groups=groups)]
    ppermute x1, waiting for transfers between devices: 1.53 us -> 0.01 us  [local(): other = lax.ppermute(mine, 'tp', [(i, i ^ 1) for i in range(parts)])]
    convert_element_type x1, other arithmetic: 0.01 us -> 0.69 us  [local(): live = (section_index < flat_exits).astype(jnp.float32)]
    pallas_call x1 -> x2, Pallas kernels: 8.05 us -> 7.5 us  [the longest x1 5.28 us: local(): pl.pallas_call(split_kernel, grid=(chips,), out_shape=pltpu.HBM((parts, w...]
  transfers between devices with their start and end apart: 2 -> 2, of which waited for: 1 -> 1; matrix products, arithmetic and copies ran while one was open for 4% -> 5% of each run, Pallas kernels for 17% -> 16%
where the time goes in v5:
time: 58.6 us; the launch traced here: 58.2 us
  starting transfers between devices  24.6 us (42%)
  Pallas kernels  15.5 us (26%)
  blocking collectives  10.8 us (18%)
  local copies, waits for them, and re-layouts  2.79 us (5%)
  waiting for transfers between devices  1.99 us (3%)
  other arithmetic  1.65 us (3%)
  between operations  0.79 us (1%)
    all_to_all x1, starting transfers between devices, spread(): return lax.all_to_all(x, axis, 0, 0, axis_index_groups=groups)  15.7 us
    all_to_all x1, blocking collectives, spread(): return lax.all_to_all(x, axis, 0, 0, axis_index_groups=groups)  10.8 us
    ppermute x1, starting transfers between devices, local(): other = lax.ppermute(mine, 'tp', [(i, i ^ 1) for i in range(parts)])  8.89 us
    pallas_call x1, Pallas kernels, local(): pl.pallas_call(split_kernel, grid=(chips,), out_shape=pltpu.HBM((parts, w...  5.28 us
    pallas_call x1, Pallas kernels, local(): pl.pallas_call(lambda *refs: finish_kernel(local_reqs, scale, *refs), out...  3.85 us
    unnamed x13, local copies, waits for them, and re-layouts  2.53 us
    pallas_call x1, Pallas kernels, local(): pl.pallas_call(half_kernel, out_shape=(pltpu.VMEM((rows, 2 * HEAD), jnp.f...  2.22 us
    all_to_all x1, waiting for transfers between devices, spread(): return lax.all_to_all(x, axis, 0, 0, axis_index_groups=groups)  1.99 us
  transfers between devices with their start and end apart: 2, of which 1 were waited for; matrix products, arithmetic and copies ran while one was open for 5% of the time, Pallas kernels for 16%

profile of v5, /device:TPU:1, one launch (start us, length us, event | category | flops | bytes accessed | tf_op | source)
XLA Modules:
  0.0 58.2 jit_solution(1662140237004018004)
XLA Ops:
  0.6 1.9 %leaving.1 = bf16[16,8,1024]{2,1,0:T(8,128)(2,1)} custom-call(s32[1]{0:T(128)} %bitcast.6.section, s32[4,16]{1,0:T(4,128)} %exits_far.1, bf16[64,1024]{1,0:T(8,128)(2,1)} %bitcast.30), custom_call_target="tpu_custom_call" | custom-call | tf_op jit(solution)/shard_map/leaving/pallas_call | solution.py:255
  2.6 15.7 %all-to-all-start = ((bf16[16,8,1024]{2,1,0:T(8,128)(2,1)}), bf16[16,8,1024]{2,1,0:T(8,128)(2,1)S(1)}, u32[]{:S(2)}, u32[]{:S(2)}) async-start(bf16[16,8,1024]{2,1,0:T(8,128)(2,1)} %leaving.1), calls=%async_computation | async-start | bytes 524288 | tf_op jit(solution)/shard_map/all_to_all | solution.py:236
  18.3 0.0 copy-start.2
  18.3 0.9 %copy-done.2 = bf16[4,1,16,1024]{3,2,1,0:T(8,128)(2,1)S(1)} copy-done((bf16[4,1,16,1024]{3,2,1,0:T(8,128)(2,1)S(1)}, bf16[4,1,16,1024]{3,2,1,0:T(8,128)(2,1)}, u32[]{:S(2)}) %copy-start.2) | copy-done | bytes 131096
  19.2 0.7 %copy-done.3 = s32[4,16]{1,0:T(4,128)S(1)} copy-done((s32[4,16]{1,0:T(4,128)S(1)}, s32[4,16]{1,0:T(4,128)}, u32[]{:S(2)}) %copy-start.3) | copy-done | bytes 280
  19.9 0.4 choose.1
  20.3 0.7 %add_convert_fusion = f32[4,16]{1,0:T(4,128)S(1)} fusion(s32[16]{0:T(128)} %refs_0_.1), kind=kLoop, calls=%fused_computation.6 | loop fusion | flops 128 | bytes 320 | tf_op jit(solution)/shard_map/convert_element_type | solution.py:285
  21.0 0.1 convert_element_type.17
  21.0 0.7 %compare_convert_fusion = f32[4,16]{1,0:T(4,128)S(1)} fusion(s32[4,16]{1,0:T(4,128)} %exits_far.1, s32[]{:T(128)} %axis_index.23), kind=kLoop, calls=%fused_computation.7 | loop fusion | flops 128 | bytes 516 | tf_op jit(solution)/shard_map/convert_element_type | solution.py:287
  21.7 0.1 reshape.71
  21.8 0.9 %copy.12 = bf16[8,8,8,128]{3,2,1,0:T(8,128)(2,1)S(1)} copy(bf16[8,8,8,128]{3,1,2,0:T(8,128)(2,1)} %bitcast.27) | data formatting | bytes 262144
  22.8 0.0 copy-start
  22.8 0.0 copy-start.4
  22.8 5.3 %split.1.weight = bf16[8,1024,256]{2,1,0:T(8,128)(2,1)} custom-call(bf16[16384,128]{1,0:T(8,128)(2,1)} %bitcast.32), custom_call_target="tpu_custom_call" | custom-call | tf_op jit(solution)/shard_map/split/pallas_call | solution.py:296
  28.1 1.6 %past.1.refs_5_ = f32[8,64,384]{2,1,0:T(8,128)S(1)} custom-call(s32[16]{0:T(128)S(1)} %copy-done.5, bf16[512,128]{1,0:T(8,128)(2,1)S(1)} %bitcast.29, bf16[16,2,128,128]{3,2,1,0:T(8,128)(2,1)S(1)} %bitcast.25), custom_call_target="tpu_custom_call" | custom-call | tf_op jit(solution)/shard_map/past/pallas_call | solution.py:306
  29.7 0.2 multiply_cosine_fusion
  29.9 0.1 maximum_bitcast_fusion
  30.0 0.1 stack_broadcast_in_dim.2
  30.1 2.0 %all-to-all-done = bf16[16,8,1024]{2,1,0:T(8,128)(2,1)S(1)} async-done(((bf16[16,8,1024]{2,1,0:T(8,128)(2,1)}), bf16[16,8,1024]{2,1,0:T(8,128)(2,1)S(1)}, u32[]{:S(2)}, u32[]{:S(2)}) %all-to-all-start) | async-done | bytes 262176 | tf_op jit(solution)/shard_map/all_to_all | solution.py:236
  32.1 0.3 place.1
  32.4 10.8 %all_to_all.10.held.refs_0_ = bf16[4,520,128]{2,1,0:T(8,128)(2,1)S(1)} all-to-all(bf16[4,520,128]{2,1,0:T(8,128)(2,1)S(1)} %place.1), channel_id=1, replica_groups={{0,2,4,6},{1,3,5,7},{8,10,12,14},{9,11,13,15},{16,18,20,22},{17,19,21,2..., dimensions={0} | all-to-all | bytes 1064960 | tf_op jit(solution)/shard_map/all_to_all | solution.py:236
  43.2 8.9 %collective-permute-start = (bf16[4,520,128]{2,1,0:T(8,128)(2,1)S(1)}, bf16[4,520,128]{2,1,0:T(8,128)(2,1)S(1)}, u32[]{:S(2)}, u32[]{:S(2)}) collective-permute-start(bf16[4,520,128]{2,1,0:T(8,128)(2,1)S(1)} %all_to_all.10.held.refs_0_), channel_id=1, source_target_pairs={{0,1},{1,0},{2,3},{3,2},{4,5},{5,4},{6,7},{7,6},{8,9},{9,8},{10,11... | collective-permute-start | bytes 1597448 | tf_op jit(solution)/shard_map/ppermute | solution.py:328
  52.1 2.2 %half.1 = (f32[64,256]{1,0:T(8,128)S(1)}, bf16[4,1024,256]{2,1,0:T(8,128)(2,1)S(1)}) custom-call(s32[1]{0:T(128)} %bitcast.9.core, bf16[4,520,128]{2,1,0:T(8,128)(2,1)S(1)} %all_to_all.10.held.refs_0_, bf16[8,1024,256]{2,1,0:T(8,128)(2,1)} %split.1.weight), custom_call_target="tpu_custom_call" | custom-call | tf_op jit(solution)/shard_map/half/pallas_call | solution.py:330
  54.3 3.9 %finish.1 = (bf16[64,1024]{1,0:T(8,128)(2,1)}, bf16[128,128]{1,0:T(8,128)(2,1)}) custom-call(bf16[4,520,128]{2,1,0:T(8,128)(2,1)S(1)} %all_to_all.10.held.refs_0_, bf16[4,520,128]{2,1,0:T(8,128)(2,1)S(1)} %collective-permute-done.refs_1_, f32[64,256]{1,0:T(8,128)S(1)} %get-tuple-element.20.refs_2_, bf16[4,1024,256]{2,1,0:T(8,128)(2,1)S(1)} %get-tuple-element.21.refs_3_, ...), custom_call_target="tpu_custom_call" | custom-call | tf_op jit(solution)/shard_map/finish/pallas_call | solution.py:345
  (11 shorter events, 0.1 us)
Async XLA Ops:
  2.6 29.5 %all-to-all-start = ((bf16[16,8,1024]{2,1,0:T(8,128)(2,1)}), bf16[16,8,1024]{2,1,0:T(8,128)(2,1)S(1)}, u32[]{:S(2)}, u32[]{:S(2)}) async-start(bf16[16,8,1024]{2,1,0:T(8,128)(2,1)} %leaving.1), calls=%async_computation | async-start | bytes 524288 | tf_op jit(solution)/shard_map/all_to_all | solution.py:236
  18.3 0.9 %copy-start.2 = (bf16[4,1,16,1024]{3,2,1,0:T(8,128)(2,1)S(1)}, bf16[4,1,16,1024]{3,2,1,0:T(8,128)(2,1)}, u32[]{:S(2)}) copy-start(bf16[4,1,16,1024]{3,2,1,0:T(8,128)(2,1)} %param.7) | copy-start | bytes 393220
  19.2 0.7 %copy-start.3 = (s32[4,16]{1,0:T(4,128)S(1)}, s32[4,16]{1,0:T(4,128)}, u32[]{:S(2)}) copy-start(s32[4,16]{1,0:T(4,128)} %exits_far.1) | copy-start | bytes 772
  22.8 5.3 %copy-start = (bf16[1,16,2,128,128]{4,3,2,1,0:T(8,128)(2,1)S(1)}, bf16[1,16,2,128,128]{4,3,2,1,0:T(8,128)(2,1)}, u32[]{:S(2)}) copy-start(bf16[1,16,2,128,128]{4,3,2,1,0:T(8,128)(2,1)} %param.11) | copy-start | bytes 3145732
  22.8 5.3 %copy-start.5 = (s32[16]{0:T(128)S(1)}, s32[16]{0:T(128)}, u32[]{:S(2)}) copy-start(s32[16]{0:T(128)} %refs_0_.1) | copy-start | bytes 196
  22.8 9.3 %copy-start.4 = (bf16[1,1024]{1,0:T(2,128)(2,1)S(1)}, bf16[1,1024]{1,0:T(2,128)(2,1)}, u32[]{:S(2)}) copy-start(bf16[1,1024]{1,0:T(2,128)(2,1)} %gain.1) | copy-start | bytes 6148
  28.1 26.2 %copy-start.1 = (bf16[4,1,16,1024]{3,2,1,0:T(8,128)(2,1)S(1)}, bf16[4,1,16,1024]{3,2,1,0:T(8,128)(2,1)}, u32[]{:S(2)}) copy-start(bf16[4,1,16,1024]{3,2,1,0:T(8,128)(2,1)} %param.10) | copy-start | bytes 393220
  43.2 11.1 %collective-permute-start = (bf16[4,520,128]{2,1,0:T(8,128)(2,1)S(1)}, bf16[4,520,128]{2,1,0:T(8,128)(2,1)S(1)}, u32[]{:S(2)}, u32[]{:S(2)}) collective-permute-start(bf16[4,520,128]{2,1,0:T(8,128)(2,1)S(1)} %all_to_all.10.held.refs_0_), channel_id=1, source_target_pairs={{0,1},{1,0},{2,3},{3,2},{4,5},{5,4},{6,7},{7,6},{8,9},{9,8},{10,11... | collective-permute-start | bytes 1597448 | tf_op jit(solution)/shard_map/ppermute | solution.py:328

commit v6 on v5

--- a/solution.py
+++ b/solution.py
@@ -201,19 +201,24 @@
     by, of = iota((rows, HEAD), 0), iota((rows, HEAD), 1)
     seen = (by % reqs == of % reqs) & (of // reqs <= by // reqs)
     live = table[2]
-    for g in range(old.shape[0]):
-        span = slice(g * HEAD, (g + 1) * HEAD)
-        scores = contract_last(queries[:, span], wide_keys) * scale
-        scores = jnp.where(seen, scores, -1e30)
+    groups = old.shape[0]
+    asked = jnp.concatenate([queries[:, g * HEAD : (g + 1) * HEAD] for g in range(groups)], axis=0)
+    scores = contract_last(asked, wide_keys)
+    fresh, kept = [], []
+    for g in range(groups):
+        score = jnp.where(seen, scores[g * rows : (g + 1) * rows] * scale, -1e30)
         old_top = old[g, :, HEAD : 2 * HEAD]
-        top = jnp.maximum(old_top, jnp.max(scores, axis=-1, keepdims=True))
+        top = jnp.maximum(old_top, jnp.max(score, axis=-1, keepdims=True))
         shrink = jnp.exp(old_top - top)
-        grown = jnp.exp(scores - top)
+        grown = jnp.exp(score - top)
         total = shrink * old[g, :, 2 * HEAD :] + jnp.sum(grown, axis=-1, keepdims=True)
         part = 1.0 / total
-        fresh = (grown * part).astype(jnp.bfloat16)
-        mixed = old[g, :, 0:HEAD] * (shrink * part) + exact(fresh, wide_values)
-        out_attn[:, span] = (mixed * live).astype(jnp.bfloat16)
+        fresh.append((grown * part).astype(jnp.bfloat16))
+        kept.append(old[g, :, 0:HEAD] * (shrink * part))
+    added = exact(jnp.concatenate(fresh, axis=0), wide_values)
+    for g in range(groups):
+        mixed = kept[g] + added[g * rows : (g + 1) * rows]
+        out_attn[:, g * HEAD : (g + 1) * HEAD] = (mixed * live).astype(jnp.bfloat16)
     to, fro = iota((2 * rows, 2 * rows), 0), iota((2 * rows, 2 * rows), 1)
     weave = as_bf16(fro == (to // 2) + rows * (to % 2))
     stacked = jnp.concatenate([new_keys, new_values], axis=0)

time: 58.6 us -> 56.6 us (0.966)
  Pallas kernels: 15.5 us -> 13.5 us
    pallas_call x1, Pallas kernels: 3.85 us -> 1.82 us  [local(): pl.pallas_call(lambda *refs: finish_kernel(local_reqs, scale, *refs), out...]
  transfers between devices with their start and end apart: 2 -> 2, of which waited for: 1 -> 1; matrix products, arithmetic and copies ran while one was open for 5% -> 5% of each run, Pallas kernels for 16% -> 17%
where the time goes in v6:
time: 56.6 us; the launch traced here: 56.2 us
  starting transfers between devices  24.6 us (43%)
  Pallas kernels  13.5 us (24%)
  blocking collectives  10.8 us (19%)
  local copies, waits for them, and re-layouts  2.79 us (5%)
  waiting for transfers between devices  1.99 us (4%)
  other arithmetic  1.65 us (3%)
  between operations  0.79 us (1%)
    all_to_all x1, starting transfers between devices, spread(): return lax.all_to_all(x, axis, 0, 0, axis_index_groups=groups)  15.7 us
    all_to_all x1, blocking collectives, spread(): return lax.all_to_all(x, axis, 0, 0, axis_index_groups=groups)  10.8 us
    ppermute x1, starting transfers between devices, local(): other = lax.ppermute(mine, 'tp', [(i, i ^ 1) for i in range(parts)])  8.89 us
    pallas_call x1, Pallas kernels, local(): pl.pallas_call(split_kernel, grid=(chips,), out_shape=pltpu.HBM((parts, w...  5.28 us
    unnamed x13, local copies, waits for them, and re-layouts  2.53 us
    pallas_call x1, Pallas kernels, local(): pl.pallas_call(half_kernel, out_shape=(pltpu.VMEM((rows, 2 * HEAD), jnp.f...  2.22 us
    all_to_all x1, waiting for transfers between devices, spread(): return lax.all_to_all(x, axis, 0, 0, axis_index_groups=groups)  1.99 us
    pallas_call x1, Pallas kernels, local(): pl.pallas_call(leaving_kernel, out_shape=pltpu.HBM((sections, slots, widt...  1.92 us
  transfers between devices with their start and end apart: 2, of which 1 were waited for; matrix products, arithmetic and copies ran while one was open for 5% of the time, Pallas kernels for 17%

profile of v6, /device:TPU:1, one launch (start us, length us, event | category | flops | bytes accessed | tf_op | source)
XLA Modules:
  0.0 56.2 jit_solution(12086248473013982839)
XLA Ops:
  0.6 1.9 %leaving.1 = bf16[16,8,1024]{2,1,0:T(8,128)(2,1)} custom-call(s32[1]{0:T(128)} %bitcast.6.section, s32[4,16]{1,0:T(4,128)} %exits_far.1, bf16[64,1024]{1,0:T(8,128)(2,1)} %bitcast.30), custom_call_target="tpu_custom_call" | custom-call | tf_op jit(solution)/shard_map/leaving/pallas_call | solution.py:260
  2.6 15.7 %all-to-all-start = ((bf16[16,8,1024]{2,1,0:T(8,128)(2,1)}), bf16[16,8,1024]{2,1,0:T(8,128)(2,1)S(1)}, u32[]{:S(2)}, u32[]{:S(2)}) async-start(bf16[16,8,1024]{2,1,0:T(8,128)(2,1)} %leaving.1), calls=%async_computation | async-start | bytes 524288 | tf_op jit(solution)/shard_map/all_to_all | solution.py:241
  18.3 0.0 copy-start.2
  18.3 0.9 %copy-done.2 = bf16[4,1,16,1024]{3,2,1,0:T(8,128)(2,1)S(1)} copy-done((bf16[4,1,16,1024]{3,2,1,0:T(8,128)(2,1)S(1)}, bf16[4,1,16,1024]{3,2,1,0:T(8,128)(2,1)}, u32[]{:S(2)}) %copy-start.2) | copy-done | bytes 131096
  19.2 0.7 %copy-done.3 = s32[4,16]{1,0:T(4,128)S(1)} copy-done((s32[4,16]{1,0:T(4,128)S(1)}, s32[4,16]{1,0:T(4,128)}, u32[]{:S(2)}) %copy-start.3) | copy-done | bytes 280
  19.9 0.4 choose.1
  20.3 0.7 %add_convert_fusion = f32[4,16]{1,0:T(4,128)S(1)} fusion(s32[16]{0:T(128)} %refs_0_.1), kind=kLoop, calls=%fused_computation.6 | loop fusion | flops 128 | bytes 320 | tf_op jit(solution)/shard_map/convert_element_type | solution.py:290
  21.0 0.1 convert_element_type.17
  21.0 0.7 %compare_convert_fusion = f32[4,16]{1,0:T(4,128)S(1)} fusion(s32[4,16]{1,0:T(4,128)} %exits_far.1, s32[]{:T(128)} %axis_index.23), kind=kLoop, calls=%fused_computation.7 | loop fusion | flops 128 | bytes 516 | tf_op jit(solution)/shard_map/convert_element_type | solution.py:292
  21.7 0.1 reshape.71
  21.8 0.9 %copy.12 = bf16[8,8,8,128]{3,2,1,0:T(8,128)(2,1)S(1)} copy(bf16[8,8,8,128]{3,1,2,0:T(8,128)(2,1)} %bitcast.27) | data formatting | bytes 262144
  22.8 0.0 copy-start
  22.8 0.0 copy-start.4
  22.8 5.3 %split.1.weight = bf16[8,1024,256]{2,1,0:T(8,128)(2,1)} custom-call(bf16[16384,128]{1,0:T(8,128)(2,1)} %bitcast.32), custom_call_target="tpu_custom_call" | custom-call | tf_op jit(solution)/shard_map/split/pallas_call | solution.py:301
  28.1 1.6 %past.1.refs_5_ = f32[8,64,384]{2,1,0:T(8,128)S(1)} custom-call(s32[16]{0:T(128)S(1)} %copy-done.5, bf16[512,128]{1,0:T(8,128)(2,1)S(1)} %bitcast.29, bf16[16,2,128,128]{3,2,1,0:T(8,128)(2,1)S(1)} %bitcast.25), custom_call_target="tpu_custom_call" | custom-call | tf_op jit(solution)/shard_map/past/pallas_call | solution.py:311
  29.7 0.2 multiply_cosine_fusion
  29.9 0.1 maximum_bitcast_fusion
  30.0 0.1 stack_broadcast_in_dim.2
  30.1 2.0 %all-to-all-done = bf16[16,8,1024]{2,1,0:T(8,128)(2,1)S(1)} async-done(((bf16[16,8,1024]{2,1,0:T(8,128)(2,1)}), bf16[16,8,1024]{2,1,0:T(8,128)(2,1)S(1)}, u32[]{:S(2)}, u32[]{:S(2)}) %all-to-all-start) | async-done | bytes 262176 | tf_op jit(solution)/shard_map/all_to_all | solution.py:241
  32.1 0.3 place.1
  32.4 10.8 %all_to_all.10.held.refs_0_ = bf16[4,520,128]{2,1,0:T(8,128)(2,1)S(1)} all-to-all(bf16[4,520,128]{2,1,0:T(8,128)(2,1)S(1)} %place.1), channel_id=1, replica_groups={{0,2,4,6},{1,3,5,7},{8,10,12,14},{9,11,13,15},{16,18,20,22},{17,19,21,2..., dimensions={0} | all-to-all | bytes 1064960 | tf_op jit(solution)/shard_map/all_to_all | solution.py:241
  43.2 8.9 %collective-permute-start = (bf16[4,520,128]{2,1,0:T(8,128)(2,1)S(1)}, bf16[4,520,128]{2,1,0:T(8,128)(2,1)S(1)}, u32[]{:S(2)}, u32[]{:S(2)}) collective-permute-start(bf16[4,520,128]{2,1,0:T(8,128)(2,1)S(1)} %all_to_all.10.held.refs_0_), channel_id=1, source_target_pairs={{0,1},{1,0},{2,3},{3,2},{4,5},{5,4},{6,7},{7,6},{8,9},{9,8},{10,11... | collective-permute-start | bytes 1597448 | tf_op jit(solution)/shard_map/ppermute | solution.py:333
  52.1 2.2 %half.1 = (f32[64,256]{1,0:T(8,128)S(1)}, bf16[4,1024,256]{2,1,0:T(8,128)(2,1)S(1)}) custom-call(s32[1]{0:T(128)} %bitcast.9.core, bf16[4,520,128]{2,1,0:T(8,128)(2,1)S(1)} %all_to_all.10.held.refs_0_, bf16[8,1024,256]{2,1,0:T(8,128)(2,1)} %split.1.weight), custom_call_target="tpu_custom_call" | custom-call | tf_op jit(solution)/shard_map/half/pallas_call | solution.py:335
  54.3 1.8 %finish.1 = (bf16[64,1024]{1,0:T(8,128)(2,1)}, bf16[128,128]{1,0:T(8,128)(2,1)}) custom-call(bf16[4,520,128]{2,1,0:T(8,128)(2,1)S(1)} %all_to_all.10.held.refs_0_, bf16[4,520,128]{2,1,0:T(8,128)(2,1)S(1)} %collective-permute-done.refs_1_, f32[64,256]{1,0:T(8,128)S(1)} %get-tuple-element.20.refs_2_, bf16[4,1024,256]{2,1,0:T(8,128)(2,1)S(1)} %get-tuple-element.21.refs_3_, ...), custom_call_target="tpu_custom_call" | custom-call | tf_op jit(solution)/shard_map/finish/pallas_call | solution.py:350
  (11 shorter events, 0.1 us)
Async XLA Ops:
  2.6 29.5 %all-to-all-start = ((bf16[16,8,1024]{2,1,0:T(8,128)(2,1)}), bf16[16,8,1024]{2,1,0:T(8,128)(2,1)S(1)}, u32[]{:S(2)}, u32[]{:S(2)}) async-start(bf16[16,8,1024]{2,1,0:T(8,128)(2,1)} %leaving.1), calls=%async_computation | async-start | bytes 524288 | tf_op jit(solution)/shard_map/all_to_all | solution.py:241
  18.3 0.9 %copy-start.2 = (bf16[4,1,16,1024]{3,2,1,0:T(8,128)(2,1)S(1)}, bf16[4,1,16,1024]{3,2,1,0:T(8,128)(2,1)}, u32[]{:S(2)}) copy-start(bf16[4,1,16,1024]{3,2,1,0:T(8,128)(2,1)} %param.7) | copy-start | bytes 393220
  19.2 0.7 %copy-start.3 = (s32[4,16]{1,0:T(4,128)S(1)}, s32[4,16]{1,0:T(4,128)}, u32[]{:S(2)}) copy-start(s32[4,16]{1,0:T(4,128)} %exits_far.1) | copy-start | bytes 772
  22.8 5.3 %copy-start = (bf16[1,16,2,128,128]{4,3,2,1,0:T(8,128)(2,1)S(1)}, bf16[1,16,2,128,128]{4,3,2,1,0:T(8,128)(2,1)}, u32[]{:S(2)}) copy-start(bf16[1,16,2,128,128]{4,3,2,1,0:T(8,128)(2,1)} %param.11) | copy-start | bytes 3145732
  22.8 5.3 %copy-start.5 = (s32[16]{0:T(128)S(1)}, s32[16]{0:T(128)}, u32[]{:S(2)}) copy-start(s32[16]{0:T(128)} %refs_0_.1) | copy-start | bytes 196
  22.8 9.3 %copy-start.4 = (bf16[1,1024]{1,0:T(2,128)(2,1)S(1)}, bf16[1,1024]{1,0:T(2,128)(2,1)}, u32[]{:S(2)}) copy-start(bf16[1,1024]{1,0:T(2,128)(2,1)} %gain.1) | copy-start | bytes 6148
  28.1 26.2 %copy-start.1 = (bf16[4,1,16,1024]{3,2,1,0:T(8,128)(2,1)S(1)}, bf16[4,1,16,1024]{3,2,1,0:T(8,128)(2,1)}, u32[]{:S(2)}) copy-start(bf16[4,1,16,1024]{3,2,1,0:T(8,128)(2,1)} %param.10) | copy-start | bytes 393220
  43.2 11.1 %collective-permute-start = (bf16[4,520,128]{2,1,0:T(8,128)(2,1)S(1)}, bf16[4,520,128]{2,1,0:T(8,128)(2,1)S(1)}, u32[]{:S(2)}, u32[]{:S(2)}) collective-permute-start(bf16[4,520,128]{2,1,0:T(8,128)(2,1)S(1)} %all_to_all.10.held.refs_0_), channel_id=1, source_target_pairs={{0,1},{1,0},{2,3},{3,2},{4,5},{5,4},{6,7},{7,6},{8,9},{9,8},{10,11... | collective-permute-start | bytes 1597448 | tf_op jit(solution)/shard_map/ppermute | solution.py:333

commit v7 on v6

--- a/solution.py
+++ b/solution.py
@@ -9,6 +9,8 @@
 HEAD = 128
 EXIT_CAP = 2
 EXTRA = 8
+TURN = 8
+CHIP_ORDER = (0,1,2,3)
 
 
 EPSILON = 1e-05
@@ -77,7 +79,8 @@
         same = layer == e
         rank = jnp.where(same, ranks(same), rank)
     gone = layer < section[0]
-    slot = layer * slots + rank.astype(jnp.int32) * steps + iota((steps, reqs), 0)
+    count = reach // slots
+    slot = ((layer + count - TURN) % count) * slots + rank.astype(jnp.int32) * steps + iota((steps, reqs), 0)
     slot = jnp.where(gone, slot, -1).astype(jnp.float32)
     spread_steps = as_bf16(iota((rows, steps), 0) // reqs == iota((rows, steps), 1))
     column = exact(spread_steps, slot.astype(jnp.bfloat16))
@@ -160,9 +163,12 @@
     chips = held.shape[0]
     blocks = weight.shape[1] // HEAD
     rows = pairs.shape[0]
-    loads = [pltpu.make_async_copy(weight.at[2 * x + core[0]], mine.at[x], sems.at[x]) for x in range(chips)]
+    loads = [
+        pltpu.make_async_copy(weight.at[2 * CHIP_ORDER[x] + core[0]], mine.at[x], sems.at[x])
+        for x in range(chips)
+    ]
     more = [
-        pltpu.make_async_copy(weight.at[2 * x + 1 - core[0]], ahead.at[x], sems.at[chips + x])
+        pltpu.make_async_copy(weight.at[2 * CHIP_ORDER[x] + 1 - core[0]], ahead.at[x], sems.at[chips + x])
         for x in range(chips)
     ]
     for load in loads + more:
@@ -271,7 +277,8 @@
         compiler_params=small(4),
         name="leaving",
     )(section_scalar, far(exits), far(own))
-    arrived = spread(outgoing, "section").reshape(sections * slots, width)
+    ring = [[(k + TURN) % sections for k in range(sections)]]
+    arrived = spread(outgoing, "section", ring).reshape(sections * slots, width)
 
     take, kept = pl.pallas_call(
         choose_kernel,
@@ -328,7 +335,7 @@
         compiler_params=small(4),
         name="place",
     )(near(take), near(kept), near(arrived), near(norm_gain))
-    same_core = [[2 * x + c for x in range(chips)] for c in range(2)]
+    same_core = [[2 * x + c for x in CHIP_ORDER] for c in range(2)]
     mine = spread(sent, "tp", same_core)
     other = lax.ppermute(mine, "tp", [(i, i ^ 1) for i in range(parts)])
 

time: 56.6 us -> 55.2 us (0.975)
  starting transfers between devices: 24.6 us -> 23 us
  blocking collectives: 10.8 us -> 12.3 us
  waiting for transfers between devices: 1.99 us -> 0.7 us
    ppermute x1, starting transfers between devices: 8.89 us -> 3.92 us  [local(): other = lax.ppermute(mine, 'tp', [(i, i ^ 1) for i in range(parts)])]
    all_to_all x1, starting transfers between devices: 15.7 us -> 19.1 us  [spread(): return lax.all_to_all(x, axis, 0, 0, axis_index_groups=groups)]
    all_to_all x1, blocking collectives: 10.8 us -> 12.3 us  [spread(): return lax.all_to_all(x, axis, 0, 0, axis_index_groups=groups)]
    all_to_all x1, waiting for transfers between devices: 1.99 us -> 0.7 us  [spread(): return lax.all_to_all(x, axis, 0, 0, axis_index_groups=groups)]
where the time goes in v7:
time: 55.2 us; the launch traced here: 54.8 us
  starting transfers between devices  23 us (42%)
  Pallas kernels  13.5 us (24%)
  blocking collectives  12.3 us (22%)
  local copies, waits for them, and re-layouts  2.79 us (5%)
  other arithmetic  1.65 us (3%)
  between operations  0.78 us (1%)
  waiting for transfers between devices  0.7 us (1%)
    all_to_all x1, starting transfers between devices, spread(): return lax.all_to_all(x, axis, 0, 0, axis_index_groups=groups)  19.1 us
    all_to_all x1, blocking collectives, spread(): return lax.all_to_all(x, axis, 0, 0, axis_index_groups=groups)  12.3 us
    pallas_call x1, Pallas kernels, local(): pl.pallas_call(split_kernel, grid=(chips,), out_shape=pltpu.HBM((parts, w...  5.28 us
    ppermute x1, starting transfers between devices, local(): other = lax.ppermute(mine, 'tp', [(i, i ^ 1) for i in range(parts)])  3.92 us
    unnamed x13, local copies, waits for them, and re-layouts  2.53 us
    pallas_call x1, Pallas kernels, local(): pl.pallas_call(half_kernel, out_shape=(pltpu.VMEM((rows, 2 * HEAD), jnp.f...  2.22 us
    pallas_call x1, Pallas kernels, local(): pl.pallas_call(leaving_kernel, out_shape=pltpu.HBM((sections, slots, widt...  1.92 us
    pallas_call x1, Pallas kernels, local(): pl.pallas_call(lambda *refs: finish_kernel(local_reqs, scale, *refs), out...  1.82 us
  transfers between devices with their start and end apart: 2, of which 1 were waited for; matrix products, arithmetic and copies ran while one was open for 5% of the time, Pallas kernels for 17%

profile of v7, /device:TPU:1, one launch (start us, length us, event | category | flops | bytes accessed | tf_op | source)
XLA Modules:
  0.0 54.8 jit_solution(11383031247018596551)
XLA Ops:
  0.6 1.9 %leaving.1 = bf16[16,8,1024]{2,1,0:T(8,128)(2,1)} custom-call(s32[1]{0:T(128)} %bitcast.6.section, s32[4,16]{1,0:T(4,128)} %exits_far.1, bf16[64,1024]{1,0:T(8,128)(2,1)} %bitcast.30), custom_call_target="tpu_custom_call" | custom-call | tf_op jit(solution)/shard_map/leaving/pallas_call | solution.py:266
  2.6 19.1 %all-to-all-start = ((bf16[16,8,1024]{2,1,0:T(8,128)(2,1)}), bf16[16,8,1024]{2,1,0:T(8,128)(2,1)S(1)}, u32[]{:S(2)}, u32[]{:S(2)}) async-start(bf16[16,8,1024]{2,1,0:T(8,128)(2,1)} %leaving.1), calls=%async_computation | async-start | bytes 524288 | tf_op jit(solution)/shard_map/all_to_all | solution.py:247
  21.7 0.9 %copy-done.2 = bf16[4,1,16,1024]{3,2,1,0:T(8,128)(2,1)S(1)} copy-done((bf16[4,1,16,1024]{3,2,1,0:T(8,128)(2,1)S(1)}, bf16[4,1,16,1024]{3,2,1,0:T(8,128)(2,1)}, u32[]{:S(2)}) %copy-start.2) | copy-done | bytes 131096
  22.6 0.7 %copy-done.3 = s32[4,16]{1,0:T(4,128)S(1)} copy-done((s32[4,16]{1,0:T(4,128)S(1)}, s32[4,16]{1,0:T(4,128)}, u32[]{:S(2)}) %copy-start.3) | copy-done | bytes 280
  23.3 0.4 choose.1
  23.7 0.7 %add_convert_fusion = f32[4,16]{1,0:T(4,128)S(1)} fusion(s32[16]{0:T(128)} %refs_0_.1), kind=kLoop, calls=%fused_computation.6 | loop fusion | flops 128 | bytes 320 | tf_op jit(solution)/shard_map/convert_element_type | solution.py:297
  24.3 0.1 convert_element_type.17
  24.4 0.7 %compare_convert_fusion = f32[4,16]{1,0:T(4,128)S(1)} fusion(s32[4,16]{1,0:T(4,128)} %exits_far.1, s32[]{:T(128)} %axis_index.23), kind=kLoop, calls=%fused_computation.7 | loop fusion | flops 128 | bytes 516 | tf_op jit(solution)/shard_map/convert_element_type | solution.py:299
  25.1 0.1 reshape.71
  25.2 0.9 %copy.12 = bf16[8,8,8,128]{3,2,1,0:T(8,128)(2,1)S(1)} copy(bf16[8,8,8,128]{3,1,2,0:T(8,128)(2,1)} %bitcast.27) | data formatting | bytes 262144
  26.1 0.0 copy-start
  26.2 0.0 copy-start.5
  26.2 0.0 copy-start.4
  26.2 5.3 %split.1.weight = bf16[8,1024,256]{2,1,0:T(8,128)(2,1)} custom-call(bf16[16384,128]{1,0:T(8,128)(2,1)} %bitcast.32), custom_call_target="tpu_custom_call" | custom-call | tf_op jit(solution)/shard_map/split/pallas_call | solution.py:308
  31.5 1.6 %past.1.refs_5_ = f32[8,64,384]{2,1,0:T(8,128)S(1)} custom-call(s32[16]{0:T(128)S(1)} %copy-done.5, bf16[512,128]{1,0:T(8,128)(2,1)S(1)} %bitcast.29, bf16[16,2,128,128]{3,2,1,0:T(8,128)(2,1)S(1)} %bitcast.25), custom_call_target="tpu_custom_call" | custom-call | tf_op jit(solution)/shard_map/past/pallas_call | solution.py:318
  33.1 0.2 multiply_cosine_fusion
  33.3 0.1 maximum_bitcast_fusion
  33.4 0.1 stack_broadcast_in_dim.2
  33.5 0.7 %all-to-all-done = bf16[16,8,1024]{2,1,0:T(8,128)(2,1)S(1)} async-done(((bf16[16,8,1024]{2,1,0:T(8,128)(2,1)}), bf16[16,8,1024]{2,1,0:T(8,128)(2,1)S(1)}, u32[]{:S(2)}, u32[]{:S(2)}) %all-to-all-start) | async-done | bytes 262176 | tf_op jit(solution)/shard_map/all_to_all | solution.py:247
  34.2 0.3 place.1
  34.5 12.3 %all_to_all.10.held.refs_0_ = bf16[4,520,128]{2,1,0:T(8,128)(2,1)S(1)} all-to-all(bf16[4,520,128]{2,1,0:T(8,128)(2,1)S(1)} %place.1), channel_id=1, replica_groups={{0,2,4,6},{1,3,5,7},{8,10,12,14},{9,11,13,15},{16,18,20,22},{17,19,21,2..., dimensions={0} | all-to-all | bytes 1064960 | tf_op jit(solution)/shard_map/all_to_all | solution.py:247
  46.8 3.9 %collective-permute-start = (bf16[4,520,128]{2,1,0:T(8,128)(2,1)S(1)}, bf16[4,520,128]{2,1,0:T(8,128)(2,1)S(1)}, u32[]{:S(2)}, u32[]{:S(2)}) collective-permute-start(bf16[4,520,128]{2,1,0:T(8,128)(2,1)S(1)} %all_to_all.10.held.refs_0_), channel_id=1, source_target_pairs={{0,1},{1,0},{2,3},{3,2},{4,5},{5,4},{6,7},{7,6},{8,9},{9,8},{10,11... | collective-permute-start | bytes 1597448 | tf_op jit(solution)/shard_map/ppermute | solution.py:340
  50.7 2.2 %half.1 = (f32[64,256]{1,0:T(8,128)S(1)}, bf16[4,1024,256]{2,1,0:T(8,128)(2,1)S(1)}) custom-call(s32[1]{0:T(128)} %bitcast.9.core, bf16[4,520,128]{2,1,0:T(8,128)(2,1)S(1)} %all_to_all.10.held.refs_0_, bf16[8,1024,256]{2,1,0:T(8,128)(2,1)} %split.1.weight), custom_call_target="tpu_custom_call" | custom-call | tf_op jit(solution)/shard_map/half/pallas_call | solution.py:342
  53.0 1.8 %finish.1 = (bf16[64,1024]{1,0:T(8,128)(2,1)}, bf16[128,128]{1,0:T(8,128)(2,1)}) custom-call(bf16[4,520,128]{2,1,0:T(8,128)(2,1)S(1)} %all_to_all.10.held.refs_0_, bf16[4,520,128]{2,1,0:T(8,128)(2,1)S(1)} %collective-permute-done.refs_1_, f32[64,256]{1,0:T(8,128)S(1)} %get-tuple-element.20.refs_2_, bf16[4,1024,256]{2,1,0:T(8,128)(2,1)S(1)} %get-tuple-element.21.refs_3_, ...), custom_call_target="tpu_custom_call" | custom-call | tf_op jit(solution)/shard_map/finish/pallas_call | solution.py:357
  (11 shorter events, 0.1 us)
Async XLA Ops:
  2.6 31.6 %all-to-all-start = ((bf16[16,8,1024]{2,1,0:T(8,128)(2,1)}), bf16[16,8,1024]{2,1,0:T(8,128)(2,1)S(1)}, u32[]{:S(2)}, u32[]{:S(2)}) async-start(bf16[16,8,1024]{2,1,0:T(8,128)(2,1)} %leaving.1), calls=%async_computation | async-start | bytes 524288 | tf_op jit(solution)/shard_map/all_to_all | solution.py:247
  21.7 0.9 %copy-start.2 = (bf16[4,1,16,1024]{3,2,1,0:T(8,128)(2,1)S(1)}, bf16[4,1,16,1024]{3,2,1,0:T(8,128)(2,1)}, u32[]{:S(2)}) copy-start(bf16[4,1,16,1024]{3,2,1,0:T(8,128)(2,1)} %param.7) | copy-start | bytes 393220
  22.6 0.7 %copy-start.3 = (s32[4,16]{1,0:T(4,128)S(1)}, s32[4,16]{1,0:T(4,128)}, u32[]{:S(2)}) copy-start(s32[4,16]{1,0:T(4,128)} %exits_far.1) | copy-start | bytes 772
  26.1 5.3 %copy-start = (bf16[1,16,2,128,128]{4,3,2,1,0:T(8,128)(2,1)S(1)}, bf16[1,16,2,128,128]{4,3,2,1,0:T(8,128)(2,1)}, u32[]{:S(2)}) copy-start(bf16[1,16,2,128,128]{4,3,2,1,0:T(8,128)(2,1)} %param.11) | copy-start | bytes 3145732
  26.2 5.3 %copy-start.5 = (s32[16]{0:T(128)S(1)}, s32[16]{0:T(128)}, u32[]{:S(2)}) copy-start(s32[16]{0:T(128)} %refs_0_.1) | copy-start | bytes 196
  26.2 8.0 %copy-start.4 = (bf16[1,1024]{1,0:T(2,128)(2,1)S(1)}, bf16[1,1024]{1,0:T(2,128)(2,1)}, u32[]{:S(2)}) copy-start(bf16[1,1024]{1,0:T(2,128)(2,1)} %gain.1) | copy-start | bytes 6148
  31.5 21.5 %copy-start.1 = (bf16[4,1,16,1024]{3,2,1,0:T(8,128)(2,1)S(1)}, bf16[4,1,16,1024]{3,2,1,0:T(8,128)(2,1)}, u32[]{:S(2)}) copy-start(bf16[4,1,16,1024]{3,2,1,0:T(8,128)(2,1)} %param.10) | copy-start | bytes 393220
  46.8 6.2 %collective-permute-start = (bf16[4,520,128]{2,1,0:T(8,128)(2,1)S(1)}, bf16[4,520,128]{2,1,0:T(8,128)(2,1)S(1)}, u32[]{:S(2)}, u32[]{:S(2)}) collective-permute-start(bf16[4,520,128]{2,1,0:T(8,128)(2,1)S(1)} %all_to_all.10.held.refs_0_), channel_id=1, source_target_pairs={{0,1},{1,0},{2,3},{3,2},{4,5},{5,4},{6,7},{7,6},{8,9},{9,8},{10,11... | collective-permute-start | bytes 1597448 | tf_op jit(solution)/shard_map/ppermute | solution.py:340
